TPU v7x, 512 devices: a whole 4x8x8 slice. The times are simulated.
512 devices in a mesh: head: 16 (over y, z_hi), seq: 32 (over x, z_lo, core).
Axes of the slice: x: 4, y: 8, z: 8 (z_hi: 2, z_lo: 4; z = z_hi * 4 + z_lo), core: 2. Of those that a mesh axis runs over, the one named last changes fastest.
Arguments:
- queries: bfloat16 [1, 32768, 8192], P(None, 'seq', 'head'), may hold values from -6 to 6
- keys: bfloat16 [1, 32768, 8192], P(None, 'seq', 'head'), may hold values from -6 to 6
- values: bfloat16 [1, 32768, 8192], P(None, 'seq', 'head'), may hold values from -60 to 60
- decay_rate: float32 [64], P('head'), may hold values from 1.5258789e-07 to 0.03
- norm_gain: float32 [8192], P('head'), may hold values from 0.25 to 1.75
- offsets: int32 [1], replicated, may hold values from 0 to 31
Outputs:
- normed: bfloat16 [1, 32768, 8192], P(None, 'seq', 'head')
All inputs are finite; a program needn't handle non-finite values.
Results may differ from a plain program's by a relative error of at most 0.0044.
Values sent between devices are 32-bit elements; how exact they have to be, the bound alone decides.
No kernel may reach another device: no remote copies, remote signals or barrier semaphores. Data moves between devices by JAX's collectives and lax.ppermute only.
A program may use at most 64 MiB of HBM per device.

v0:
```python
import jax
import jax.numpy as jnp
from jax import lax
from jax.sharding import PartitionSpec as P

epsilon = 1e-05


def from_behind(shard, axis, by):
    count = lax.axis_size(axis)
    return lax.ppermute(shard, axis, [(i, (i + by) % count) for i in range(count)])


def body(queries, keys, values, decay_rate, norm_gain, offsets):
    seq_count, block_len, columns = queries.shape
    heads_dev = decay_rate.shape[0]
    head_size = columns // heads_dev
    shaped = (seq_count, block_len, heads_dev, head_size)
    query_heads = queries.reshape(shaped)
    key_heads = keys.reshape(shaped)
    value_heads = values.reshape(shaped)
    places = jnp.arange(block_len).astype(jnp.float32)
    distance = places[:, None] - places[None, :]
    within = (
        jnp.exp(-decay_rate[:, None, None] * jnp.maximum(distance, 0.0)[None])
        * (distance >= 0.0).astype(jnp.float32)[None]
    )
    scores = jnp.einsum(
        "sihd,sjhd->shij", query_heads, key_heads, preferred_element_type=jnp.float32
    )
    weights = (scores * within[None]).astype(jnp.bfloat16)
    inner_part = jnp.einsum(
        "shij,sjhd->sihd", weights, value_heads, preferred_element_type=jnp.float32
    )
    key_scale = jnp.exp(-decay_rate[None, :] * (block_len - 1.0 - places[:, None]))
    decayed_keys = (key_heads.astype(jnp.float32) * key_scale[None, :, :, None]).astype(
        jnp.bfloat16
    )
    local_state = jnp.einsum(
        "sjhd,sjhe->shde", decayed_keys, value_heads, preferred_element_type=jnp.float32
    )
    group_decay = jnp.exp(-decay_rate * block_len)[None, :, None, None]
    cycle_size = lax.axis_size("seq")
    loop_place = lax.axis_index("seq")
    group_index = jnp.mod(loop_place - offsets, cycle_size)

    def follows(stride):
        return (group_index >= stride).astype(jnp.float32)[:, None, None, None]

    def advance(turn_index, incoming):
        outgoing = local_state + group_decay * incoming
        return follows(1) * from_behind(outgoing, "seq", 1)

    incoming = lax.fori_loop(0, cycle_size - 1, advance, jnp.zeros_like(local_state))
    query_scale = jnp.exp(-decay_rate[None, :] * (places[:, None] + 1.0))
    scaled_queries = query_heads.astype(jnp.float32) * query_scale[None, :, :, None]
    carried_part = jnp.einsum(
        "sihd,shde->sihe", scaled_queries, incoming, precision=lax.Precision.HIGHEST
    )
    attended = (inner_part + carried_part).reshape(seq_count, block_len, columns)
    squares = jnp.sum(attended * attended, axis=-1)
    sum_squares = lax.psum(squares, "head")
    features_all = columns * lax.axis_size("head")
    inv_rms = lax.rsqrt(sum_squares / features_all + epsilon)
    return (attended * inv_rms[..., None] * norm_gain).astype(jnp.bfloat16)


def solution(mesh):
    in_specs = (
        P(None, "seq", "head"),
        P(None, "seq", "head"),
        P(None, "seq", "head"),
        P("head"),
        P("head"),
        P(),
    )
    out_specs = P(None, "seq", "head")
    return jax.shard_map(body, mesh=mesh, in_specs=in_specs, out_specs=out_specs, check_vma=False)
```

profile of v0, /device:TPU:8, one launch (start us, length us, event | category | flops | bytes accessed | tf_op | source)
XLA Modules:
  0.0 450.2 jit_solution(8367281808237662304)
XLA Ops:
  7.3 365.9 %while.13 = (s32[]{:T(128)}, f32[1,4,128,128]{3,2,1,0:T(8,128)S(1)}, pred[1]{0:T(512)(128)(4,1)}, f32[1,4,1,1]{1,3,2,0:T(1,128)S(1)}, f32[1,4,128,128]{3,2,1,0:T(8,128)S(1)}, /*index=5*/s32[]{:T(128)}, s32[]{:T(128)}) while((s32[]{:T(128)}, f32[1,4,128,128]{3,2,1,0:T(8,128)S(1)}, pred[1]{0:T(512)(128)(4,1)}, ...), condition=%wide.region_1.2_spmd.clone, body=%wide.region_0.1_spmd.clone.sunk | while | flops 262148 | bytes 2359448 | solution.py:54
  9.3 11.6 %collective-permute-done = f32[1,4,128,128]{3,2,1,0:T(8,128)S(1)} collective-permute-done((f32[1,4,128,128]{3,2,1,0:T(8,128)S(1)}, f32[1,4,128,128]{3,2,1,0:T(8,128)S(1)}, u32[]{:S(2)}, u32[]{:S(2)}) %collective-permute-start) | collective-permute-done | bytes 262176 | tf_op jit(solution)/shard_map/while/body/eval_jaxpr/ppermute | solution.py:11
  23.0 9.7 %collective-permute-done = f32[1,4,128,128]{3,2,1,0:T(8,128)S(1)} collective-permute-done((f32[1,4,128,128]{3,2,1,0:T(8,128)S(1)}, f32[1,4,128,128]{3,2,1,0:T(8,128)S(1)}, u32[]{:S(2)}, u32[]{:S(2)}) %collective-permute-start) | collective-permute-done | bytes 262176 | tf_op jit(solution)/shard_map/while/body/eval_jaxpr/ppermute | solution.py:11
  34.8 9.7 %collective-permute-done = f32[1,4,128,128]{3,2,1,0:T(8,128)S(1)} collective-permute-done((f32[1,4,128,128]{3,2,1,0:T(8,128)S(1)}, f32[1,4,128,128]{3,2,1,0:T(8,128)S(1)}, u32[]{:S(2)}, u32[]{:S(2)}) %collective-permute-start) | collective-permute-done | bytes 262176 | tf_op jit(solution)/shard_map/while/body/eval_jaxpr/ppermute | solution.py:11
  46.5 9.7 %collective-permute-done = f32[1,4,128,128]{3,2,1,0:T(8,128)S(1)} collective-permute-done((f32[1,4,128,128]{3,2,1,0:T(8,128)S(1)}, f32[1,4,128,128]{3,2,1,0:T(8,128)S(1)}, u32[]{:S(2)}, u32[]{:S(2)}) %collective-permute-start) | collective-permute-done | bytes 262176 | tf_op jit(solution)/shard_map/while/body/eval_jaxpr/ppermute | solution.py:11
  58.2 9.7 %collective-permute-done = f32[1,4,128,128]{3,2,1,0:T(8,128)S(1)} collective-permute-done((f32[1,4,128,128]{3,2,1,0:T(8,128)S(1)}, f32[1,4,128,128]{3,2,1,0:T(8,128)S(1)}, u32[]{:S(2)}, u32[]{:S(2)}) %collective-permute-start) | collective-permute-done | bytes 262176 | tf_op jit(solution)/shard_map/while/body/eval_jaxpr/ppermute | solution.py:11
  70.0 9.7 %collective-permute-done = f32[1,4,128,128]{3,2,1,0:T(8,128)S(1)} collective-permute-done((f32[1,4,128,128]{3,2,1,0:T(8,128)S(1)}, f32[1,4,128,128]{3,2,1,0:T(8,128)S(1)}, u32[]{:S(2)}, u32[]{:S(2)}) %collective-permute-start) | collective-permute-done | bytes 262176 | tf_op jit(solution)/shard_map/while/body/eval_jaxpr/ppermute | solution.py:11
  81.7 9.7 %collective-permute-done = f32[1,4,128,128]{3,2,1,0:T(8,128)S(1)} collective-permute-done((f32[1,4,128,128]{3,2,1,0:T(8,128)S(1)}, f32[1,4,128,128]{3,2,1,0:T(8,128)S(1)}, u32[]{:S(2)}, u32[]{:S(2)}) %collective-permute-start) | collective-permute-done | bytes 262176 | tf_op jit(solution)/shard_map/while/body/eval_jaxpr/ppermute | solution.py:11
  93.4 9.7 %collective-permute-done = f32[1,4,128,128]{3,2,1,0:T(8,128)S(1)} collective-permute-done((f32[1,4,128,128]{3,2,1,0:T(8,128)S(1)}, f32[1,4,128,128]{3,2,1,0:T(8,128)S(1)}, u32[]{:S(2)}, u32[]{:S(2)}) %collective-permute-start) | collective-permute-done | bytes 262176 | tf_op jit(solution)/shard_map/while/body/eval_jaxpr/ppermute | solution.py:11
  105.2 9.7 %collective-permute-done = f32[1,4,128,128]{3,2,1,0:T(8,128)S(1)} collective-permute-done((f32[1,4,128,128]{3,2,1,0:T(8,128)S(1)}, f32[1,4,128,128]{3,2,1,0:T(8,128)S(1)}, u32[]{:S(2)}, u32[]{:S(2)}) %collective-permute-start) | collective-permute-done | bytes 262176 | tf_op jit(solution)/shard_map/while/body/eval_jaxpr/ppermute | solution.py:11
  116.9 9.7 %collective-permute-done = f32[1,4,128,128]{3,2,1,0:T(8,128)S(1)} collective-permute-done((f32[1,4,128,128]{3,2,1,0:T(8,128)S(1)}, f32[1,4,128,128]{3,2,1,0:T(8,128)S(1)}, u32[]{:S(2)}, u32[]{:S(2)}) %collective-permute-start) | collective-permute-done | bytes 262176 | tf_op jit(solution)/shard_map/while/body/eval_jaxpr/ppermute | solution.py:11
  128.6 9.7 %collective-permute-done = f32[1,4,128,128]{3,2,1,0:T(8,128)S(1)} collective-permute-done((f32[1,4,128,128]{3,2,1,0:T(8,128)S(1)}, f32[1,4,128,128]{3,2,1,0:T(8,128)S(1)}, u32[]{:S(2)}, u32[]{:S(2)}) %collective-permute-start) | collective-permute-done | bytes 262176 | tf_op jit(solution)/shard_map/while/body/eval_jaxpr/ppermute | solution.py:11
  140.4 9.7 %collective-permute-done = f32[1,4,128,128]{3,2,1,0:T(8,128)S(1)} collective-permute-done((f32[1,4,128,128]{3,2,1,0:T(8,128)S(1)}, f32[1,4,128,128]{3,2,1,0:T(8,128)S(1)}, u32[]{:S(2)}, u32[]{:S(2)}) %collective-permute-start) | collective-permute-done | bytes 262176 | tf_op jit(solution)/shard_map/while/body/eval_jaxpr/ppermute | solution.py:11
  163.9 9.7 %collective-permute-done = f32[1,4,128,128]{3,2,1,0:T(8,128)S(1)} collective-permute-done((f32[1,4,128,128]{3,2,1,0:T(8,128)S(1)}, f32[1,4,128,128]{3,2,1,0:T(8,128)S(1)}, u32[]{:S(2)}, u32[]{:S(2)}) %collective-permute-start) | collective-permute-done | bytes 262176 | tf_op jit(solution)/shard_map/while/body/eval_jaxpr/ppermute | solution.py:11
  175.6 9.7 %collective-permute-done = f32[1,4,128,128]{3,2,1,0:T(8,128)S(1)} collective-permute-done((f32[1,4,128,128]{3,2,1,0:T(8,128)S(1)}, f32[1,4,128,128]{3,2,1,0:T(8,128)S(1)}, u32[]{:S(2)}, u32[]{:S(2)}) %collective-permute-start) | collective-permute-done | bytes 262176 | tf_op jit(solution)/shard_map/while/body/eval_jaxpr/ppermute | solution.py:11
  187.3 9.7 %collective-permute-done = f32[1,4,128,128]{3,2,1,0:T(8,128)S(1)} collective-permute-done((f32[1,4,128,128]{3,2,1,0:T(8,128)S(1)}, f32[1,4,128,128]{3,2,1,0:T(8,128)S(1)}, u32[]{:S(2)}, u32[]{:S(2)}) %collective-permute-start) | collective-permute-done | bytes 262176 | tf_op jit(solution)/shard_map/while/body/eval_jaxpr/ppermute | solution.py:11
  234.3 9.7 %collective-permute-done = f32[1,4,128,128]{3,2,1,0:T(8,128)S(1)} collective-permute-done((f32[1,4,128,128]{3,2,1,0:T(8,128)S(1)}, f32[1,4,128,128]{3,2,1,0:T(8,128)S(1)}, u32[]{:S(2)}, u32[]{:S(2)}) %collective-permute-start) | collective-permute-done | bytes 262176 | tf_op jit(solution)/shard_map/while/body/eval_jaxpr/ppermute | solution.py:11
  246.0 9.7 %collective-permute-done = f32[1,4,128,128]{3,2,1,0:T(8,128)S(1)} collective-permute-done((f32[1,4,128,128]{3,2,1,0:T(8,128)S(1)}, f32[1,4,128,128]{3,2,1,0:T(8,128)S(1)}, u32[]{:S(2)}, u32[]{:S(2)}) %collective-permute-start) | collective-permute-done | bytes 262176 | tf_op jit(solution)/shard_map/while/body/eval_jaxpr/ppermute | solution.py:11
  257.7 9.7 %collective-permute-done = f32[1,4,128,128]{3,2,1,0:T(8,128)S(1)} collective-permute-done((f32[1,4,128,128]{3,2,1,0:T(8,128)S(1)}, f32[1,4,128,128]{3,2,1,0:T(8,128)S(1)}, u32[]{:S(2)}, u32[]{:S(2)}) %collective-permute-start) | collective-permute-done | bytes 262176 | tf_op jit(solution)/shard_map/while/body/eval_jaxpr/ppermute | solution.py:11
  304.7 9.7 %collective-permute-done = f32[1,4,128,128]{3,2,1,0:T(8,128)S(1)} collective-permute-done((f32[1,4,128,128]{3,2,1,0:T(8,128)S(1)}, f32[1,4,128,128]{3,2,1,0:T(8,128)S(1)}, u32[]{:S(2)}, u32[]{:S(2)}) %collective-permute-start) | collective-permute-done | bytes 262176 | tf_op jit(solution)/shard_map/while/body/eval_jaxpr/ppermute | solution.py:11
  316.4 9.7 %collective-permute-done = f32[1,4,128,128]{3,2,1,0:T(8,128)S(1)} collective-permute-done((f32[1,4,128,128]{3,2,1,0:T(8,128)S(1)}, f32[1,4,128,128]{3,2,1,0:T(8,128)S(1)}, u32[]{:S(2)}, u32[]{:S(2)}) %collective-permute-start) | collective-permute-done | bytes 262176 | tf_op jit(solution)/shard_map/while/body/eval_jaxpr/ppermute | solution.py:11
  328.1 9.7 %collective-permute-done = f32[1,4,128,128]{3,2,1,0:T(8,128)S(1)} collective-permute-done((f32[1,4,128,128]{3,2,1,0:T(8,128)S(1)}, f32[1,4,128,128]{3,2,1,0:T(8,128)S(1)}, u32[]{:S(2)}, u32[]{:S(2)}) %collective-permute-start) | collective-permute-done | bytes 262176 | tf_op jit(solution)/shard_map/while/body/eval_jaxpr/ppermute | solution.py:11
  363.4 9.8 %collective-permute-done = f32[1,4,128,128]{3,2,1,0:T(8,128)S(1)} collective-permute-done((f32[1,4,128,128]{3,2,1,0:T(8,128)S(1)}, f32[1,4,128,128]{3,2,1,0:T(8,128)S(1)}, u32[]{:S(2)}, u32[]{:S(2)}) %collective-permute-start) | collective-permute-done | bytes 262176 | tf_op jit(solution)/shard_map/while/body/eval_jaxpr/ppermute | solution.py:11
  391.5 54.0 %psum.7 = f32[1,1024]{1,0:T(1,128)S(1)} all-reduce(f32[1,1024]{1,0:T(1,128)S(1)} %bitcast.33), channel_id=1, replica_groups=mesh['head'=16,'seq'=32] {'head'}, use_global_device_ids=true, to_apply=%region_3.4 | all-reduce | flops 1024 | bytes 8192 | tf_op jit(solution)/shard_map/psum | solution.py:62
  (124 shorter events, 179.5 us)
Async XLA Ops:
  7.4 13.6 %collective-permute-start = (f32[1,4,128,128]{3,2,1,0:T(8,128)S(1)}, f32[1,4,128,128]{3,2,1,0:T(8,128)S(1)}, u32[]{:S(2)}, u32[]{:S(2)}) collective-permute-start(f32[1,4,128,128]{3,2,1,0:T(8,128)S(1)} %fusion.21), channel_id=1, source_target_pairs={{0,1},{1,2},{2,3},{3,4},{4,5},{5,6},{6,7},{7,8},{8,9},{9,10},{10,1... | collective-permute-start | bytes 786440 | tf_op jit(solution)/shard_map/while/body/eval_jaxpr/ppermute | solution.py:11
  21.1 11.6 %collective-permute-start = (f32[1,4,128,128]{3,2,1,0:T(8,128)S(1)}, f32[1,4,128,128]{3,2,1,0:T(8,128)S(1)}, u32[]{:S(2)}, u32[]{:S(2)}) collective-permute-start(f32[1,4,128,128]{3,2,1,0:T(8,128)S(1)} %fusion.21), channel_id=1, source_target_pairs={{0,1},{1,2},{2,3},{3,4},{4,5},{5,6},{6,7},{7,8},{8,9},{9,10},{10,1... | collective-permute-start | bytes 786440 | tf_op jit(solution)/shard_map/while/body/eval_jaxpr/ppermute | solution.py:11
  32.8 11.6 %collective-permute-start = (f32[1,4,128,128]{3,2,1,0:T(8,128)S(1)}, f32[1,4,128,128]{3,2,1,0:T(8,128)S(1)}, u32[]{:S(2)}, u32[]{:S(2)}) collective-permute-start(f32[1,4,128,128]{3,2,1,0:T(8,128)S(1)} %fusion.21), channel_id=1, source_target_pairs={{0,1},{1,2},{2,3},{3,4},{4,5},{5,6},{6,7},{7,8},{8,9},{9,10},{10,1... | collective-permute-start | bytes 786440 | tf_op jit(solution)/shard_map/while/body/eval_jaxpr/ppermute | solution.py:11
  44.6 11.6 %collective-permute-start = (f32[1,4,128,128]{3,2,1,0:T(8,128)S(1)}, f32[1,4,128,128]{3,2,1,0:T(8,128)S(1)}, u32[]{:S(2)}, u32[]{:S(2)}) collective-permute-start(f32[1,4,128,128]{3,2,1,0:T(8,128)S(1)} %fusion.21), channel_id=1, source_target_pairs={{0,1},{1,2},{2,3},{3,4},{4,5},{5,6},{6,7},{7,8},{8,9},{9,10},{10,1... | collective-permute-start | bytes 786440 | tf_op jit(solution)/shard_map/while/body/eval_jaxpr/ppermute | solution.py:11
  56.3 11.6 %collective-permute-start = (f32[1,4,128,128]{3,2,1,0:T(8,128)S(1)}, f32[1,4,128,128]{3,2,1,0:T(8,128)S(1)}, u32[]{:S(2)}, u32[]{:S(2)}) collective-permute-start(f32[1,4,128,128]{3,2,1,0:T(8,128)S(1)} %fusion.21), channel_id=1, source_target_pairs={{0,1},{1,2},{2,3},{3,4},{4,5},{5,6},{6,7},{7,8},{8,9},{9,10},{10,1... | collective-permute-start | bytes 786440 | tf_op jit(solution)/shard_map/while/body/eval_jaxpr/ppermute | solution.py:11
  68.0 11.6 %collective-permute-start = (f32[1,4,128,128]{3,2,1,0:T(8,128)S(1)}, f32[1,4,128,128]{3,2,1,0:T(8,128)S(1)}, u32[]{:S(2)}, u32[]{:S(2)}) collective-permute-start(f32[1,4,128,128]{3,2,1,0:T(8,128)S(1)} %fusion.21), channel_id=1, source_target_pairs={{0,1},{1,2},{2,3},{3,4},{4,5},{5,6},{6,7},{7,8},{8,9},{9,10},{10,1... | collective-permute-start | bytes 786440 | tf_op jit(solution)/shard_map/while/body/eval_jaxpr/ppermute | solution.py:11
  79.8 11.6 %collective-permute-start = (f32[1,4,128,128]{3,2,1,0:T(8,128)S(1)}, f32[1,4,128,128]{3,2,1,0:T(8,128)S(1)}, u32[]{:S(2)}, u32[]{:S(2)}) collective-permute-start(f32[1,4,128,128]{3,2,1,0:T(8,128)S(1)} %fusion.21), channel_id=1, source_target_pairs={{0,1},{1,2},{2,3},{3,4},{4,5},{5,6},{6,7},{7,8},{8,9},{9,10},{10,1... | collective-permute-start | bytes 786440 | tf_op jit(solution)/shard_map/while/body/eval_jaxpr/ppermute | solution.py:11
  91.5 11.6 %collective-permute-start = (f32[1,4,128,128]{3,2,1,0:T(8,128)S(1)}, f32[1,4,128,128]{3,2,1,0:T(8,128)S(1)}, u32[]{:S(2)}, u32[]{:S(2)}) collective-permute-start(f32[1,4,128,128]{3,2,1,0:T(8,128)S(1)} %fusion.21), channel_id=1, source_target_pairs={{0,1},{1,2},{2,3},{3,4},{4,5},{5,6},{6,7},{7,8},{8,9},{9,10},{10,1... | collective-permute-start | bytes 786440 | tf_op jit(solution)/shard_map/while/body/eval_jaxpr/ppermute | solution.py:11
  103.2 11.6 %collective-permute-start = (f32[1,4,128,128]{3,2,1,0:T(8,128)S(1)}, f32[1,4,128,128]{3,2,1,0:T(8,128)S(1)}, u32[]{:S(2)}, u32[]{:S(2)}) collective-permute-start(f32[1,4,128,128]{3,2,1,0:T(8,128)S(1)} %fusion.21), channel_id=1, source_target_pairs={{0,1},{1,2},{2,3},{3,4},{4,5},{5,6},{6,7},{7,8},{8,9},{9,10},{10,1... | collective-permute-start | bytes 786440 | tf_op jit(solution)/shard_map/while/body/eval_jaxpr/ppermute | solution.py:11
  115.0 11.6 %collective-permute-start = (f32[1,4,128,128]{3,2,1,0:T(8,128)S(1)}, f32[1,4,128,128]{3,2,1,0:T(8,128)S(1)}, u32[]{:S(2)}, u32[]{:S(2)}) collective-permute-start(f32[1,4,128,128]{3,2,1,0:T(8,128)S(1)} %fusion.21), channel_id=1, source_target_pairs={{0,1},{1,2},{2,3},{3,4},{4,5},{5,6},{6,7},{7,8},{8,9},{9,10},{10,1... | collective-permute-start | bytes 786440 | tf_op jit(solution)/shard_map/while/body/eval_jaxpr/ppermute | solution.py:11
  126.7 11.6 %collective-permute-start = (f32[1,4,128,128]{3,2,1,0:T(8,128)S(1)}, f32[1,4,128,128]{3,2,1,0:T(8,128)S(1)}, u32[]{:S(2)}, u32[]{:S(2)}) collective-permute-start(f32[1,4,128,128]{3,2,1,0:T(8,128)S(1)} %fusion.21), channel_id=1, source_target_pairs={{0,1},{1,2},{2,3},{3,4},{4,5},{5,6},{6,7},{7,8},{8,9},{9,10},{10,1... | collective-permute-start | bytes 786440 | tf_op jit(solution)/shard_map/while/body/eval_jaxpr/ppermute | solution.py:11
  138.4 11.6 %collective-permute-start = (f32[1,4,128,128]{3,2,1,0:T(8,128)S(1)}, f32[1,4,128,128]{3,2,1,0:T(8,128)S(1)}, u32[]{:S(2)}, u32[]{:S(2)}) collective-permute-start(f32[1,4,128,128]{3,2,1,0:T(8,128)S(1)} %fusion.21), channel_id=1, source_target_pairs={{0,1},{1,2},{2,3},{3,4},{4,5},{5,6},{6,7},{7,8},{8,9},{9,10},{10,1... | collective-permute-start | bytes 786440 | tf_op jit(solution)/shard_map/while/body/eval_jaxpr/ppermute | solution.py:11
  150.2 11.6 %collective-permute-start = (f32[1,4,128,128]{3,2,1,0:T(8,128)S(1)}, f32[1,4,128,128]{3,2,1,0:T(8,128)S(1)}, u32[]{:S(2)}, u32[]{:S(2)}) collective-permute-start(f32[1,4,128,128]{3,2,1,0:T(8,128)S(1)} %fusion.21), channel_id=1, source_target_pairs={{0,1},{1,2},{2,3},{3,4},{4,5},{5,6},{6,7},{7,8},{8,9},{9,10},{10,1... | collective-permute-start | bytes 786440 | tf_op jit(solution)/shard_map/while/body/eval_jaxpr/ppermute | solution.py:11
  161.9 11.6 %collective-permute-start = (f32[1,4,128,128]{3,2,1,0:T(8,128)S(1)}, f32[1,4,128,128]{3,2,1,0:T(8,128)S(1)}, u32[]{:S(2)}, u32[]{:S(2)}) collective-permute-start(f32[1,4,128,128]{3,2,1,0:T(8,128)S(1)} %fusion.21), channel_id=1, source_target_pairs={{0,1},{1,2},{2,3},{3,4},{4,5},{5,6},{6,7},{7,8},{8,9},{9,10},{10,1... | collective-permute-start | bytes 786440 | tf_op jit(solution)/shard_map/while/body/eval_jaxpr/ppermute | solution.py:11
  173.7 11.6 %collective-permute-start = (f32[1,4,128,128]{3,2,1,0:T(8,128)S(1)}, f32[1,4,128,128]{3,2,1,0:T(8,128)S(1)}, u32[]{:S(2)}, u32[]{:S(2)}) collective-permute-start(f32[1,4,128,128]{3,2,1,0:T(8,128)S(1)} %fusion.21), channel_id=1, source_target_pairs={{0,1},{1,2},{2,3},{3,4},{4,5},{5,6},{6,7},{7,8},{8,9},{9,10},{10,1... | collective-permute-start | bytes 786440 | tf_op jit(solution)/shard_map/while/body/eval_jaxpr/ppermute | solution.py:11
  185.4 11.6 %collective-permute-start = (f32[1,4,128,128]{3,2,1,0:T(8,128)S(1)}, f32[1,4,128,128]{3,2,1,0:T(8,128)S(1)}, u32[]{:S(2)}, u32[]{:S(2)}) collective-permute-start(f32[1,4,128,128]{3,2,1,0:T(8,128)S(1)} %fusion.21), channel_id=1, source_target_pairs={{0,1},{1,2},{2,3},{3,4},{4,5},{5,6},{6,7},{7,8},{8,9},{9,10},{10,1... | collective-permute-start | bytes 786440 | tf_op jit(solution)/shard_map/while/body/eval_jaxpr/ppermute | solution.py:11
  197.1 11.6 %collective-permute-start = (f32[1,4,128,128]{3,2,1,0:T(8,128)S(1)}, f32[1,4,128,128]{3,2,1,0:T(8,128)S(1)}, u32[]{:S(2)}, u32[]{:S(2)}) collective-permute-start(f32[1,4,128,128]{3,2,1,0:T(8,128)S(1)} %fusion.21), channel_id=1, source_target_pairs={{0,1},{1,2},{2,3},{3,4},{4,5},{5,6},{6,7},{7,8},{8,9},{9,10},{10,1... | collective-permute-start | bytes 786440 | tf_op jit(solution)/shard_map/while/body/eval_jaxpr/ppermute | solution.py:11
  208.9 11.6 %collective-permute-start = (f32[1,4,128,128]{3,2,1,0:T(8,128)S(1)}, f32[1,4,128,128]{3,2,1,0:T(8,128)S(1)}, u32[]{:S(2)}, u32[]{:S(2)}) collective-permute-start(f32[1,4,128,128]{3,2,1,0:T(8,128)S(1)} %fusion.21), channel_id=1, source_target_pairs={{0,1},{1,2},{2,3},{3,4},{4,5},{5,6},{6,7},{7,8},{8,9},{9,10},{10,1... | collective-permute-start | bytes 786440 | tf_op jit(solution)/shard_map/while/body/eval_jaxpr/ppermute | solution.py:11
  220.6 11.6 %collective-permute-start = (f32[1,4,128,128]{3,2,1,0:T(8,128)S(1)}, f32[1,4,128,128]{3,2,1,0:T(8,128)S(1)}, u32[]{:S(2)}, u32[]{:S(2)}) collective-permute-start(f32[1,4,128,128]{3,2,1,0:T(8,128)S(1)} %fusion.21), channel_id=1, source_target_pairs={{0,1},{1,2},{2,3},{3,4},{4,5},{5,6},{6,7},{7,8},{8,9},{9,10},{10,1... | collective-permute-start | bytes 786440 | tf_op jit(solution)/shard_map/while/body/eval_jaxpr/ppermute | solution.py:11
  232.3 11.6 %collective-permute-start = (f32[1,4,128,128]{3,2,1,0:T(8,128)S(1)}, f32[1,4,128,128]{3,2,1,0:T(8,128)S(1)}, u32[]{:S(2)}, u32[]{:S(2)}) collective-permute-start(f32[1,4,128,128]{3,2,1,0:T(8,128)S(1)} %fusion.21), channel_id=1, source_target_pairs={{0,1},{1,2},{2,3},{3,4},{4,5},{5,6},{6,7},{7,8},{8,9},{9,10},{10,1... | collective-permute-start | bytes 786440 | tf_op jit(solution)/shard_map/while/body/eval_jaxpr/ppermute | solution.py:11
  244.1 11.6 %collective-permute-start = (f32[1,4,128,128]{3,2,1,0:T(8,128)S(1)}, f32[1,4,128,128]{3,2,1,0:T(8,128)S(1)}, u32[]{:S(2)}, u32[]{:S(2)}) collective-permute-start(f32[1,4,128,128]{3,2,1,0:T(8,128)S(1)} %fusion.21), channel_id=1, source_target_pairs={{0,1},{1,2},{2,3},{3,4},{4,5},{5,6},{6,7},{7,8},{8,9},{9,10},{10,1... | collective-permute-start | bytes 786440 | tf_op jit(solution)/shard_map/while/body/eval_jaxpr/ppermute | solution.py:11
  255.8 11.6 %collective-permute-start = (f32[1,4,128,128]{3,2,1,0:T(8,128)S(1)}, f32[1,4,128,128]{3,2,1,0:T(8,128)S(1)}, u32[]{:S(2)}, u32[]{:S(2)}) collective-permute-start(f32[1,4,128,128]{3,2,1,0:T(8,128)S(1)} %fusion.21), channel_id=1, source_target_pairs={{0,1},{1,2},{2,3},{3,4},{4,5},{5,6},{6,7},{7,8},{8,9},{9,10},{10,1... | collective-permute-start | bytes 786440 | tf_op jit(solution)/shard_map/while/body/eval_jaxpr/ppermute | solution.py:11
  302.7 11.6 %collective-permute-start = (f32[1,4,128,128]{3,2,1,0:T(8,128)S(1)}, f32[1,4,128,128]{3,2,1,0:T(8,128)S(1)}, u32[]{:S(2)}, u32[]{:S(2)}) collective-permute-start(f32[1,4,128,128]{3,2,1,0:T(8,128)S(1)} %fusion.21), channel_id=1, source_target_pairs={{0,1},{1,2},{2,3},{3,4},{4,5},{5,6},{6,7},{7,8},{8,9},{9,10},{10,1... | collective-permute-start | bytes 786440 | tf_op jit(solution)/shard_map/while/body/eval_jaxpr/ppermute | solution.py:11
  361.4 11.7 %collective-permute-start = (f32[1,4,128,128]{3,2,1,0:T(8,128)S(1)}, f32[1,4,128,128]{3,2,1,0:T(8,128)S(1)}, u32[]{:S(2)}, u32[]{:S(2)}) collective-permute-start(f32[1,4,128,128]{3,2,1,0:T(8,128)S(1)} %fusion.21), channel_id=1, source_target_pairs={{0,1},{1,2},{2,3},{3,4},{4,5},{5,6},{6,7},{7,8},{8,9},{9,10},{10,1... | collective-permute-start | bytes 786440 | tf_op jit(solution)/shard_map/while/body/eval_jaxpr/ppermute | solution.py:11
  (10 other events, 150.2 us)
where the time goes:
time: 451 us; the launch traced here: 450 us
  waiting for transfers between devices  302 us (67%)
  starting transfers between devices  59.5 us (13%)
  blocking collectives  54 us (12%)
  matrix products  15.3 us (3%)
  other arithmetic  11.8 us (3%)
  local copies, waits for them, and re-layouts  5.88 us (1%)
    ppermute x31, waiting for transfers between devices, from_behind(): lax.ppermute(shard, axis, [(i, (i + by) % count) for i in range(count)])  302 us
    ppermute x31, starting transfers between devices, from_behind(): lax.ppermute(shard, axis, [(i, (i + by) % count) for i in range(count)])  59.5 us
    psum x1, blocking collectives, body(): sum_squares = lax.psum(squares, 'head')  54 us
    dot_general x1, matrix products, body(): jnp.einsum('shij,sjhd->sihd', weights, value_heads, preferred_element_typ...  9.53 us
  transfers between devices with their start and end apart: 31, of which 31 were waited for; matrix products, arithmetic and copies ran while one was open for 0% of the time, Pallas kernels for 0%

commit v1 on v0

v1 whole, which is shorter than its diff:
```python
import functools

import jax
import jax.numpy as jnp
from jax import lax
from jax.experimental import pallas as pl
from jax.experimental.pallas import tpu as pltpu
from jax.sharding import PartitionSpec as P

epsilon = 1e-05
CHUNK = 256
LANES = 128
F32 = jnp.float32
BF16 = jnp.bfloat16
PARAMS = pltpu.CompilerParams(vmem_limit_bytes=16 * 2**20)


def dot(left, right, left_dim, right_dim):
    return lax.dot_general(
        left, right, (((left_dim,), (right_dim,)), ((), ())), preferred_element_type=F32
    )


def rows_of(shape):
    return lax.broadcasted_iota(jnp.int32, shape, 0).astype(F32)


def times_state(query, state):
    high = state.astype(BF16)
    low = (state - high.astype(F32)).astype(BF16)
    return dot(
        jnp.concatenate([query, query], axis=1), jnp.concatenate([high, low], axis=0), 1, 0
    )


def local_kernel(rate_ref, k_ref, v_ref, out_ref):
    rate = rate_ref[pl.program_id(0)]
    block_len, head_size = k_ref.shape
    places = rows_of((block_len, head_size))
    scale = jnp.exp(-rate * (block_len - 1.0 - places))
    decayed = (k_ref[...].astype(F32) * scale).astype(BF16)
    out_ref[0] = dot(decayed, v_ref[...], 0, 0)


def inner_kernel(rate_ref, q_ref, k_ref, v_ref, out_ref):
    rate = rate_ref[pl.program_id(0)]
    block_len, head_size = q_ref.shape
    chunk = min(CHUNK, block_len)
    square = (chunk, chunk)
    distance = rows_of(square) - lax.broadcasted_iota(jnp.int32, square, 1).astype(F32)
    within = jnp.where(distance >= 0.0, jnp.exp(-rate * jnp.maximum(distance, 0.0)), 0.0)
    places = rows_of((chunk, head_size))
    key_scale = jnp.exp(-rate * (chunk - 1.0 - places))
    query_scale = jnp.exp(-rate * (places + 1.0))
    chunk_decay = jnp.exp(jnp.full((head_size, head_size), -rate * chunk, F32))
    state = None
    for start in range(0, block_len, chunk):
        here = pl.ds(start, chunk)
        query, key, value = q_ref[here, :], k_ref[here, :], v_ref[here, :]
        weights = (dot(query, key, 1, 1) * within).astype(BF16)
        result = dot(weights, value, 1, 0)
        if state is not None:
            result = result + query_scale * times_state(query, state)
        out_ref[here, :] = result
        if start + chunk < block_len:
            decayed = (key.astype(F32) * key_scale).astype(BF16)
            added = dot(decayed, value, 0, 0)
            state = added if state is None else chunk_decay * state + added


def scan_kernel(block_len, rate_ref, place_ref, offset_ref, in_ref, out_ref):
    count, rows, lanes = in_ref.shape
    heads = rate_ref.shape[0]
    rate = rate_ref[place_ref[0] * heads // count]
    decay = jnp.exp(jnp.full((rows, lanes), -rate * block_len, F32))
    state = jnp.zeros((rows, lanes), F32)
    place = offset_ref[0]
    for _ in range(count):
        out_ref[place] = state
        state = decay * state + in_ref[place]
        place = jnp.where(place + 1 == count, 0, place + 1)


def attend_kernel(rate_ref, q_ref, inner_ref, state_ref, out_ref, square_ref):
    step = pl.program_id(0)
    rows, columns = q_ref.shape
    heads, head_size, _ = state_ref.shape
    places = rows_of((rows, head_size)) + (step * rows + 1).astype(F32)
    total = jnp.zeros((rows, head_size), F32)
    for head in range(heads):
        here = pl.ds(head * head_size, head_size)
        scale = jnp.exp(-rate_ref[head] * places)
        attended = inner_ref[:, here] + scale * times_state(q_ref[:, here], state_ref[head])
        out_ref[:, here] = attended
        total = total + attended * attended
    for part in range(rows // LANES):
        piece = total[part * LANES : (part + 1) * LANES]
        square_ref[0, part : part + 1, :] = jnp.sum(piece.T, axis=0, keepdims=True)


def norm_kernel(features_all, attended_ref, squares_ref, gain_ref, out_ref):
    rows = attended_ref.shape[0]
    total = jnp.sum(squares_ref[:, 0], axis=0)
    inv_rms = lax.rsqrt(total / features_all + epsilon)
    for part in range(rows // LANES):
        column = jnp.broadcast_to(inv_rms[part : part + 1], (LANES, LANES)).T[:, :1]
        here = pl.ds(part * LANES, LANES)
        out_ref[here, :] = (attended_ref[here, :] * column * gain_ref[...]).astype(BF16)


def body(queries, keys, values, decay_rate, norm_gain, offsets):
    seq_count, block_len, columns = queries.shape
    heads = decay_rate.shape[0]
    head_size = columns // heads
    seq_size = lax.axis_size("seq")
    head_parts = lax.axis_size("head")
    queries, keys, values = (x.reshape(block_len, columns) for x in (queries, keys, values))
    smem = pl.BlockSpec(memory_space=pltpu.SMEM)
    by_head = pl.BlockSpec((block_len, head_size), lambda h: (0, h))
    state_type = jax.ShapeDtypeStruct((heads, head_size, head_size), F32)
    wide_type = jax.ShapeDtypeStruct((block_len, columns), F32)

    local_state = pl.pallas_call(
        local_kernel,
        grid=(heads,),
        in_specs=[smem, by_head, by_head],
        out_specs=pl.BlockSpec((1, head_size, head_size), lambda h: (h, 0, 0)),
        out_shape=state_type,
        name="local_state",
        compiler_params=PARAMS,
        cost_estimate=pl.CostEstimate(
            flops=2 * block_len * columns * head_size,
            bytes_accessed=4 * block_len * columns + 4 * columns * head_size,
            transcendentals=block_len * columns,
        ),
    )(decay_rate, keys, values)

    piece_rows = columns // seq_size
    pieces = lax.all_to_all(
        local_state.reshape(seq_size, piece_rows, head_size), "seq", 0, 0, tiled=True
    )
    inner = pl.pallas_call(
        inner_kernel,
        grid=(heads,),
        in_specs=[smem, by_head, by_head, by_head],
        out_specs=by_head,
        out_shape=wide_type,
        name="inner",
        compiler_params=PARAMS,
        cost_estimate=pl.CostEstimate(
            flops=2 * block_len * columns * (2 * CHUNK + 3 * head_size),
            bytes_accessed=10 * block_len * columns,
            transcendentals=CHUNK * CHUNK * heads,
        ),
    )(decay_rate, queries, keys, values)

    place = lax.axis_index("seq").astype(jnp.int32).reshape(1)
    vmem = pl.BlockSpec(memory_space=pltpu.VMEM)
    prefixes = pl.pallas_call(
        functools.partial(scan_kernel, float(block_len)),
        in_specs=[smem, smem, smem, vmem],
        out_specs=vmem,
        out_shape=jax.ShapeDtypeStruct(pieces.shape, F32),
        name="scan",
        compiler_params=PARAMS,
    )(decay_rate, place, offsets, pieces)
    incoming = lax.all_to_all(prefixes, "seq", 0, 0, tiled=True).reshape(state_type.shape)

    steps = block_len // CHUNK
    by_rows = pl.BlockSpec((CHUNK, columns), lambda i: (i, 0))
    parts = CHUNK // LANES
    attended, squares = pl.pallas_call(
        attend_kernel,
        grid=(steps,),
        in_specs=[smem, by_rows, by_rows, pl.BlockSpec(state_type.shape, lambda i: (0, 0, 0))],
        out_specs=[by_rows, pl.BlockSpec((1, parts, LANES), lambda i: (i, 0, 0))],
        out_shape=[wide_type, jax.ShapeDtypeStruct((steps, parts, LANES), F32)],
        name="attend",
        compiler_params=PARAMS,
    )(decay_rate, queries, inner, incoming)

    squares = squares.reshape(1, block_len // LANES, LANES)
    gathered = lax.all_to_all(
        jnp.broadcast_to(squares, (head_parts, block_len // LANES, LANES)), "head", 0, 0, tiled=True
    )
    normed = pl.pallas_call(
        functools.partial(norm_kernel, float(columns * head_parts)),
        grid=(steps,),
        in_specs=[
            by_rows,
            pl.BlockSpec((head_parts, 1, parts, LANES), lambda i: (0, i, 0, 0)),
            pl.BlockSpec((1, columns), lambda i: (0, 0)),
        ],
        out_specs=by_rows,
        out_shape=jax.ShapeDtypeStruct((block_len, columns), BF16),
        name="norm",
        compiler_params=PARAMS,
    )(attended, gathered.reshape(head_parts, steps, parts, LANES), norm_gain.reshape(1, columns))
    return normed.reshape(seq_count, block_len, columns)


def solution(mesh):
    in_specs = (
        P(None, "seq", "head"),
        P(None, "seq", "head"),
        P(None, "seq", "head"),
        P("head"),
        P("head"),
        P(),
    )
    out_specs = P(None, "seq", "head")
    return jax.shard_map(body, mesh=mesh, in_specs=in_specs, out_specs=out_specs, check_vma=False)
```

time: 451 us -> 75.3 us (0.17)
  the two profiles are of different devices: /device:TPU:8 before, /device:TPU:1 now
where the time goes in v1:
time: 75.3 us; the launch traced here: 74.9 us
  blocking collectives  24.5 us (33%)
  starting transfers between devices  15 us (20%)
  Pallas kernels  13.9 us (18%)
  waiting for transfers between devices  13.9 us (18%)
  local copies, waits for them, and re-layouts  6.8 us (9%)
    all_to_all x1, blocking collectives, body(): lax.all_to_all(jnp.broadcast_to(squares, (head_parts, block_len // LANES,...  24.5 us
    all_to_all x1, starting transfers between devices, body(): lax.all_to_all(local_state.reshape(seq_size, piece_rows, head_size), 'seq...  11.4 us
    all_to_all x1, waiting for transfers between devices, body(): lax.all_to_all(local_state.reshape(seq_size, piece_rows, head_size), 'seq...  10.6 us
    unnamed x18, local copies, waits for them, and re-layouts  6.8 us
    pallas_call x1, Pallas kernels, body(): pl.pallas_call(inner_kernel, grid=(heads,), in_specs=[smem, by_head, by_h...  5.44 us
    all_to_all x1, starting transfers between devices, body(): lax.all_to_all(prefixes, 'seq', 0, 0, tiled=True).reshape(state_type.shape)  3.66 us
    all_to_all x1, waiting for transfers between devices, body(): lax.all_to_all(prefixes, 'seq', 0, 0, tiled=True).reshape(state_type.shape)  3.27 us
    pallas_call x1, Pallas kernels, body(): pl.pallas_call(local_kernel, grid=(heads,), in_specs=[smem, by_head, by_h...  3.05 us
  transfers between devices with their start and end apart: 2, of which 2 were waited for; matrix products, arithmetic and copies ran while one was open for 0% of the time, Pallas kernels for 7%

profile of v1, /device:TPU:1, one launch (start us, length us, event | category | flops | bytes accessed | tf_op | source)
XLA Modules:
  0.0 74.9 jit_solution(5825605832547565866)
XLA Ops:
  0.0 0.0 copy-start
  0.0 1.2 %copy-done = bf16[1,1024,512]{2,1,0:T(8,128)(2,1)S(1)} copy-done((bf16[1,1024,512]{2,1,0:T(8,128)(2,1)S(1)}, bf16[1,1024,512]{2,1,0:T(8,128)(2,1)}, u32[]{:S(2)}) %copy-start) | copy-done | bytes 1048600
  1.2 0.0 copy-start.2
  1.2 1.2 %copy-done.2 = bf16[1,1024,512]{2,1,0:T(8,128)(2,1)S(1)} copy-done((bf16[1,1024,512]{2,1,0:T(8,128)(2,1)S(1)}, bf16[1,1024,512]{2,1,0:T(8,128)(2,1)}, u32[]{:S(2)}) %copy-start.2) | copy-done | bytes 1048600
  2.5 0.0 copy-start.6
  2.5 0.7 copy-done.6
  3.1 0.0 copy-start.1
  3.1 3.0 %local_state.1 = f32[4,128,128]{2,1,0:T(8,128)} custom-call(f32[4]{0:T(128)S(1)} %copy-done.6, bf16[1024,512]{1,0:T(8,128)(2,1)S(1)} %bitcast.10, bf16[1024,512]{1,0:T(8,128)(2,1)S(1)} %bitcast.12), custom_call_target="tpu_custom_call" | custom-call | flops 134217728 | bytes 2359296 | tf_op jit(solution)/shard_map/local_state/pallas_call | solution.py:123
  6.2 11.4 %all-to-all-start = ((f32[32,16,128]{2,1,0:T(8,128)}), f32[32,16,128]{2,1,0:T(8,128)S(1)}, u32[]{:S(2)}, u32[]{:S(2)}) async-start(f32[32,16,128]{2,1,0:T(8,128)} %bitcast.4), calls=%async_computation | async-start | bytes 524288 | tf_op jit(solution)/shard_map/all_to_all | solution.py:139
  18.2 10.6 %all-to-all-done.in_ref = f32[32,16,128]{2,1,0:T(8,128)S(1)} async-done(((f32[32,16,128]{2,1,0:T(8,128)}), f32[32,16,128]{2,1,0:T(8,128)S(1)}, u32[]{:S(2)}, u32[]{:S(2)}) %all-to-all-start) | async-done | bytes 262176 | tf_op jit(solution)/shard_map/all_to_all | solution.py:139
  28.8 0.0 copy-done.7
  28.8 1.3 %scan.1 = f32[32,16,128]{2,1,0:T(8,128)} custom-call(f32[4]{0:T(128)S(1)} %copy-done.7, s32[1]{0:T(128)} %bitcast.3.place_ref, s32[1]{0:T(128)S(6)} %copy.7.offset_ref, f32[32,16,128]{2,1,0:T(8,128)S(1)} %all-to-all-done.in_ref), custom_call_target="tpu_custom_call" | custom-call | tf_op jit(solution)/shard_map/scan/pallas_call | solution.py:159
  30.1 3.7 %all-to-all-start.1 = ((f32[32,16,128]{2,1,0:T(8,128)}), f32[32,16,128]{2,1,0:T(8,128)S(1)}, u32[]{:S(2)}, u32[]{:S(2)}) async-start(f32[32,16,128]{2,1,0:T(8,128)} %scan.1), calls=%async_computation.1 | async-start | bytes 524288 | tf_op jit(solution)/shard_map/all_to_all | solution.py:167
  33.8 0.0 copy-done.1
  33.8 0.0 copy-start.3
  33.8 1.2 %copy-done.3 = bf16[1,1024,512]{2,1,0:T(8,128)(2,1)S(1)} copy-done((bf16[1,1024,512]{2,1,0:T(8,128)(2,1)S(1)}, bf16[1,1024,512]{2,1,0:T(8,128)(2,1)}, u32[]{:S(2)}) %copy-start.3) | copy-done | bytes 1048600
  35.0 1.2 %copy-done.4 = bf16[1,1024,512]{2,1,0:T(8,128)(2,1)S(1)} copy-done((bf16[1,1024,512]{2,1,0:T(8,128)(2,1)S(1)}, bf16[1,1024,512]{2,1,0:T(8,128)(2,1)}, u32[]{:S(2)}) %copy-start.4) | copy-done | bytes 1048600
  36.3 5.4 %inner.1.inner_ref = f32[1024,512]{1,0:T(8,128)S(1)} custom-call(f32[4]{0:T(128)S(1)} %copy-done.7, bf16[1024,512]{1,0:T(8,128)(2,1)S(1)} %bitcast.14, bf16[1024,512]{1,0:T(8,128)(2,1)S(1)} %bitcast.11, bf16[1024,512]{1,0:T(8,128)(2,1)S(1)} %bitcast.13), custom_call_target="tpu_custom_call" | custom-call | flops 939524096 | bytes 5242880 | tf_op jit(solution)/shard_map/inner/pallas_call | solution.py:142
  41.7 3.3 %all-to-all-done.1 = f32[32,16,128]{2,1,0:T(8,128)S(1)} async-done(((f32[32,16,128]{2,1,0:T(8,128)}), f32[32,16,128]{2,1,0:T(8,128)S(1)}, u32[]{:S(2)}, u32[]{:S(2)}) %all-to-all-start.1) | async-done | bytes 262176 | tf_op jit(solution)/shard_map/all_to_all | solution.py:167
  45.0 1.2 %copy-done.5 = bf16[1,1024,512]{2,1,0:T(8,128)(2,1)S(1)} copy-done((bf16[1,1024,512]{2,1,0:T(8,128)(2,1)S(1)}, bf16[1,1024,512]{2,1,0:T(8,128)(2,1)}, u32[]{:S(2)}) %copy-start.5) | copy-done | bytes 1048600
  46.2 2.0 %attend.1 = (f32[1024,512]{1,0:T(8,128)S(1)}, f32[4,2,128]{2,1,0:T(2,128)S(1)}) custom-call(f32[4]{0:T(128)S(1)} %copy-done.7, bf16[1024,512]{1,0:T(8,128)(2,1)S(1)} %bitcast.15, f32[1024,512]{1,0:T(8,128)S(1)} %inner.1.inner_ref, f32[4,128,128]{2,1,0:T(8,128)S(1)} %bitcast.16), custom_call_target="tpu_custom_call" | custom-call | tf_op jit(solution)/shard_map/attend/pallas_call | solution.py:172
  48.3 24.5 %all_to_all.15 = f32[16,8,128]{2,1,0:T(8,128)S(1)} all-to-all(f32[16,8,128]{2,1,0:T(8,128)S(1)} %broadcast_in_dim.8), channel_id=1, replica_groups=mesh['head'=16,'seq'=32] {'head'}, dimensions={0} | all-to-all | bytes 131072 | tf_op jit(solution)/shard_map/all_to_all | solution.py:183
  72.8 0.0 copy-done.8
  72.8 2.1 %norm.1 = bf16[1024,512]{1,0:T(8,128)(2,1)} custom-call(f32[1024,512]{1,0:T(8,128)S(1)} %get-tuple-element.7.attended_ref, f32[16,4,2,128]{3,2,1,0:T(2,128)S(1)} %bitcast.17, f32[1,512]{1,0:T(1,128)S(1)} %bitcast.19), custom_call_target="tpu_custom_call" | custom-call | tf_op jit(solution)/shard_map/norm/pallas_call | solution.py:186
  (5 shorter events, 0.0 us)
Async XLA Ops:
  0.0 28.8 %copy-start.7 = (f32[4]{0:T(128)S(1)}, f32[4]{0:T(128)}, u32[]{:S(2)}) copy-start(f32[4]{0:T(128)} %rate_ref.7) | copy-start | bytes 52
  0.0 1.2 %copy-start = (bf16[1,1024,512]{2,1,0:T(8,128)(2,1)S(1)}, bf16[1,1024,512]{2,1,0:T(8,128)(2,1)}, u32[]{:S(2)}) copy-start(bf16[1,1024,512]{2,1,0:T(8,128)(2,1)} %param.7) | copy-start | bytes 3145732
  1.2 1.2 %copy-start.2 = (bf16[1,1024,512]{2,1,0:T(8,128)(2,1)S(1)}, bf16[1,1024,512]{2,1,0:T(8,128)(2,1)}, u32[]{:S(2)}) copy-start(bf16[1,1024,512]{2,1,0:T(8,128)(2,1)} %param.8) | copy-start | bytes 3145732
  2.5 0.7 copy-start.6
  3.1 30.7 %copy-start.1 = (bf16[1,1024,512]{2,1,0:T(8,128)(2,1)S(1)}, bf16[1,1024,512]{2,1,0:T(8,128)(2,1)}, u32[]{:S(2)}) copy-start(bf16[1,1024,512]{2,1,0:T(8,128)(2,1)} %param.7) | copy-start | bytes 3145732
  6.2 22.6 %all-to-all-start = ((f32[32,16,128]{2,1,0:T(8,128)}), f32[32,16,128]{2,1,0:T(8,128)S(1)}, u32[]{:S(2)}, u32[]{:S(2)}) async-start(f32[32,16,128]{2,1,0:T(8,128)} %bitcast.4), calls=%async_computation | async-start | bytes 524288 | tf_op jit(solution)/shard_map/all_to_all | solution.py:139
  30.1 14.9 %all-to-all-start.1 = ((f32[32,16,128]{2,1,0:T(8,128)}), f32[32,16,128]{2,1,0:T(8,128)S(1)}, u32[]{:S(2)}, u32[]{:S(2)}) async-start(f32[32,16,128]{2,1,0:T(8,128)} %scan.1), calls=%async_computation.1 | async-start | bytes 524288 | tf_op jit(solution)/shard_map/all_to_all | solution.py:167
  33.8 1.2 %copy-start.3 = (bf16[1,1024,512]{2,1,0:T(8,128)(2,1)S(1)}, bf16[1,1024,512]{2,1,0:T(8,128)(2,1)}, u32[]{:S(2)}) copy-start(bf16[1,1024,512]{2,1,0:T(8,128)(2,1)} %param.8) | copy-start | bytes 3145732
  35.0 1.2 %copy-start.4 = (bf16[1,1024,512]{2,1,0:T(8,128)(2,1)S(1)}, bf16[1,1024,512]{2,1,0:T(8,128)(2,1)}, u32[]{:S(2)}) copy-start(bf16[1,1024,512]{2,1,0:T(8,128)(2,1)} %param.6) | copy-start | bytes 3145732
  36.3 36.5 %copy-start.8 = (f32[512]{0:T(512)S(1)}, f32[512]{0:T(512)}, u32[]{:S(2)}) copy-start(f32[512]{0:T(512)} %param.10) | copy-start | bytes 6148
  45.0 1.2 %copy-start.5 = (bf16[1,1024,512]{2,1,0:T(8,128)(2,1)S(1)}, bf16[1,1024,512]{2,1,0:T(8,128)(2,1)}, u32[]{:S(2)}) copy-start(bf16[1,1024,512]{2,1,0:T(8,128)(2,1)} %param.6) | copy-start | bytes 3145732

commit v2 on v1

v2 whole, which is shorter than its diff:
```python
import functools

import jax
import jax.numpy as jnp
from jax import lax
from jax.experimental import pallas as pl
from jax.experimental.pallas import tpu as pltpu
from jax.sharding import PartitionSpec as P

epsilon = 1e-05
CHUNK = 256
LANES = 128
F32 = jnp.float32
BF16 = jnp.bfloat16
PARAMS = pltpu.CompilerParams(vmem_limit_bytes=16 * 2**20)


def dot(left, right, left_dim, right_dim):
    return lax.dot_general(
        left, right, (((left_dim,), (right_dim,)), ((), ())), preferred_element_type=F32
    )


def rows_of(shape):
    return lax.broadcasted_iota(jnp.int32, shape, 0).astype(F32)


def on_diagonal():
    square = (LANES, LANES)
    return lax.broadcasted_iota(jnp.int32, square, 0) == lax.broadcasted_iota(jnp.int32, square, 1)


def times_state(query, state):
    high = state.astype(BF16)
    low = (state - high.astype(F32)).astype(BF16)
    return dot(
        jnp.concatenate([query, query], axis=1), jnp.concatenate([high, low], axis=0), 1, 0
    )


def head_copies(refs, bufs, sems):
    heads, _, head_size = bufs[0].shape
    copies = []
    for head in range(heads):
        here = pl.ds(head * head_size, head_size)
        row = [
            pltpu.make_async_copy(ref.at[:, here], buf.at[head], sems.at[n, head])
            for n, (ref, buf) in enumerate(zip(refs, bufs))
        ]
        for copy in row:
            copy.start()
        copies.append(row)
    return copies


def local_kernel(rate_hbm, k_hbm, v_hbm, out_ref, rates, k_buf, v_buf, sems, rate_sem):
    rate_copy = pltpu.make_async_copy(rate_hbm, rates, rate_sem)
    rate_copy.start()
    copies = head_copies((k_hbm, v_hbm), (k_buf, v_buf), sems)
    heads, block_len, head_size = k_buf.shape
    chunk = min(CHUNK, block_len)
    places = rows_of((chunk, head_size))
    rate_copy.wait()
    for head in range(heads):
        rate = rates[head]
        scale = jnp.exp(-rate * (chunk - 1.0 - places))
        chunk_decay = jnp.exp(jnp.full((chunk, head_size), -rate * chunk, F32))
        for copy in copies[head]:
            copy.wait()
        pieces = []
        for start in reversed(range(0, block_len, chunk)):
            key = k_buf[head, start : start + chunk, :]
            pieces.append((key.astype(F32) * scale).astype(BF16))
            scale = scale * chunk_decay
        out_ref[head] = dot(jnp.concatenate(pieces[::-1], axis=0), v_buf[head], 0, 0)


def inner_kernel(
    rate_hbm, q_hbm, k_hbm, v_hbm, out_ref, query_ref, wide_ref,
    rates, q_buf, k_buf, v_buf, sems, rate_sem,
):
    rate_copy = pltpu.make_async_copy(rate_hbm, rates, rate_sem)
    rate_copy.start()
    copies = head_copies((q_hbm, k_hbm, v_hbm), (q_buf, k_buf, v_buf), sems)
    heads, block_len, head_size = q_buf.shape
    chunk = min(CHUNK, block_len)
    square = (chunk, chunk)
    distance = rows_of(square) - lax.broadcasted_iota(jnp.int32, square, 1).astype(F32)
    places = rows_of((chunk, head_size))
    rate_copy.wait()
    for head in range(heads):
        rate = rates[head]
        columns = pl.ds(head * head_size, head_size)
        within = jnp.where(distance >= 0.0, jnp.exp(-rate * jnp.maximum(distance, 0.0)), 0.0)
        key_scale = jnp.exp(-rate * (chunk - 1.0 - places))
        query_scale = jnp.exp(-rate * (places + 1.0))
        chunk_decay = jnp.exp(jnp.full((head_size, head_size), -rate * chunk, F32))
        wide_ref[head] = jnp.full(wide_ref.shape[1:], -rate, F32)
        for copy in copies[head]:
            copy.wait()
        state = None
        for start in range(0, block_len, chunk):
            here = pl.ds(start, chunk)
            query, key, value = q_buf[head, here, :], k_buf[head, here, :], v_buf[head, here, :]
            weights = (dot(query, key, 1, 1) * within).astype(BF16)
            result = dot(weights, value, 1, 0)
            if state is not None:
                result = result + query_scale * times_state(query, state)
            out_ref[here, columns] = result
            query_ref[here, columns] = query
            if start + chunk < block_len:
                decayed = (key.astype(F32) * key_scale).astype(BF16)
                added = dot(decayed, value, 0, 0)
                state = added if state is None else chunk_decay * state + added


def scan_kernel(block_len, wide_ref, offset_ref, in_ref, out_ref):
    count, rows, lanes = in_ref.shape
    heads = wide_ref.shape[0]
    decay = jnp.exp(wide_ref[lax.axis_index("seq") * heads // count] * block_len)
    state = jnp.zeros((rows, lanes), F32)
    place = offset_ref[0]
    for _ in range(count):
        out_ref[place] = state
        state = decay * state + in_ref[place]
        place = jnp.where(place + 1 == count, 0, place + 1)


def attend_kernel(query_ref, inner_ref, wide_ref, state_ref, out_ref, square_ref):
    heads, head_size, _ = state_ref.shape
    block_len = query_ref.shape[0]
    places = rows_of((LANES, head_size)) + 1.0
    states, scales, steps = [], [], []
    for head in range(heads):
        minus_rate = wide_ref[head, 0:1, :]
        scales.append(jnp.exp(minus_rate * places))
        steps.append(jnp.exp(minus_rate * LANES))
        state = state_ref[head]
        high = state.astype(BF16)
        low = (state - high.astype(F32)).astype(BF16)
        states.append(jnp.concatenate([high, low], axis=0))
    diagonal = on_diagonal()
    for start in range(0, block_len, LANES):
        here = pl.ds(start, LANES)
        total = jnp.zeros((LANES, head_size), F32)
        for head in range(heads):
            columns = pl.ds(head * head_size, head_size)
            query = query_ref[here, columns]
            carried = dot(jnp.concatenate([query, query], axis=1), states[head], 1, 0)
            attended = inner_ref[here, columns] + scales[head] * carried
            scales[head] = scales[head] * steps[head]
            out_ref[here, columns] = attended
            total = total + attended * attended
        sums = jnp.where(diagonal, jnp.sum(total, axis=1, keepdims=True), 0.0)
        square_ref[pl.ds(start // LANES, 1), :] = jnp.sum(sums, axis=0, keepdims=True)


def norm_kernel(features_all, attended_ref, squares_ref, gain_ref, out_hbm, out_buf, sems):
    inv_rms = lax.rsqrt(jnp.sum(squares_ref[...], axis=0) / features_all + epsilon)
    diagonal = on_diagonal()
    copies = []
    for part in range(inv_rms.shape[0]):
        column = jnp.sum(jnp.where(diagonal, inv_rms[part : part + 1], 0.0), axis=1, keepdims=True)
        here = pl.ds(part * LANES, LANES)
        out_buf[here, :] = (attended_ref[here, :] * column * gain_ref[...]).astype(BF16)
        copies.append(pltpu.make_async_copy(out_buf.at[here], out_hbm.at[here], sems.at[part]))
        copies[-1].start()
    for copy in copies:
        copy.wait()


def body(queries, keys, values, decay_rate, norm_gain, offsets):
    seq_count, block_len, columns = queries.shape
    heads = decay_rate.shape[0]
    head_size = columns // heads
    seq_size = lax.axis_size("seq")
    head_parts = lax.axis_size("head")
    queries, keys, values, decay_rate = (
        pltpu.with_memory_space_constraint(x, pltpu.HBM)
        for x in (*(x.reshape(block_len, columns) for x in (queries, keys, values)), decay_rate)
    )
    smem = pl.BlockSpec(memory_space=pltpu.SMEM)
    vmem = pl.BlockSpec(memory_space=pltpu.VMEM)
    hbm = pl.BlockSpec(memory_space=pltpu.HBM)
    state_type = jax.ShapeDtypeStruct((heads, head_size, head_size), F32)
    wide_type = jax.ShapeDtypeStruct((block_len, columns), F32)
    piece_rows = columns // seq_size
    parts = block_len // LANES
    buffer = pltpu.VMEM((heads, block_len, head_size), BF16)
    rates = pltpu.SMEM((heads,), F32)

    local_state = pl.pallas_call(
        local_kernel,
        in_specs=[hbm] * 3,
        out_specs=vmem,
        out_shape=state_type,
        scratch_shapes=[rates, buffer, buffer, pltpu.SemaphoreType.DMA((2, heads)), pltpu.SemaphoreType.DMA],
        name="local_state",
        compiler_params=PARAMS,
        cost_estimate=pl.CostEstimate(
            flops=2 * block_len * columns * head_size,
            bytes_accessed=4 * block_len * columns + 4 * columns * head_size,
            transcendentals=block_len * columns,
        ),
    )(decay_rate, keys, values)

    pieces = lax.all_to_all(
        local_state.reshape(seq_size, piece_rows, head_size), "seq", 0, 0, tiled=True
    )
    inner, query_copy, wide_rates = pl.pallas_call(
        inner_kernel,
        in_specs=[hbm] * 4,
        out_specs=[vmem] * 3,
        out_shape=[
            wide_type,
            jax.ShapeDtypeStruct((block_len, columns), BF16),
            jax.ShapeDtypeStruct((heads, piece_rows, head_size), F32),
        ],
        scratch_shapes=[
            rates, buffer, buffer, buffer, pltpu.SemaphoreType.DMA((3, heads)), pltpu.SemaphoreType.DMA,
        ],
        name="inner",
        compiler_params=PARAMS,
        cost_estimate=pl.CostEstimate(
            flops=2 * block_len * columns * (2 * CHUNK + 3 * head_size),
            bytes_accessed=16 * block_len * columns,
            transcendentals=CHUNK * CHUNK * heads,
        ),
    )(decay_rate, queries, keys, values)

    prefixes = pl.pallas_call(
        functools.partial(scan_kernel, float(block_len)),
        in_specs=[vmem, smem, vmem],
        out_specs=vmem,
        out_shape=jax.ShapeDtypeStruct(pieces.shape, F32),
        name="scan",
        compiler_params=PARAMS,
    )(wide_rates, offsets, pieces)
    incoming = lax.all_to_all(prefixes, "seq", 0, 0, tiled=True).reshape(state_type.shape)

    attended, squares = pl.pallas_call(
        attend_kernel,
        in_specs=[vmem] * 4,
        out_specs=[vmem] * 2,
        out_shape=[wide_type, jax.ShapeDtypeStruct((parts, LANES), F32)],
        name="attend",
        compiler_params=PARAMS,
    )(query_copy, inner, wide_rates, incoming)

    gathered = lax.all_to_all(
        jnp.broadcast_to(squares, (head_parts, parts, LANES)), "head", 0, 0, tiled=True
    )
    normed = pl.pallas_call(
        functools.partial(norm_kernel, float(columns * head_parts)),
        in_specs=[vmem] * 3,
        out_specs=hbm,
        out_shape=jax.ShapeDtypeStruct((block_len, columns), BF16),
        scratch_shapes=[pltpu.VMEM((block_len, columns), BF16), pltpu.SemaphoreType.DMA((parts,))],
        name="norm",
        compiler_params=PARAMS,
    )(attended, gathered, norm_gain.reshape(1, columns))
    return normed.reshape(seq_count, block_len, columns)


def solution(mesh):
    in_specs = (
        P(None, "seq", "head"),
        P(None, "seq", "head"),
        P(None, "seq", "head"),
        P("head"),
        P("head"),
        P(),
    )
    out_specs = P(None, "seq", "head")
    return jax.shard_map(body, mesh=mesh, in_specs=in_specs, out_specs=out_specs, check_vma=False)
```

time: 75.3 us -> 67.1 us (0.89)
  blocking collectives: 24.5 us -> 39.1 us
  waiting for transfers between devices: 13.9 us -> 5.21 us
  local copies, waits for them, and re-layouts: 6.8 us -> 0.01 us
  starting transfers between devices: 15 us -> 11.4 us
  Pallas kernels: 13.9 us -> 10.4 us
    all_to_all x1 -> x2, blocking collectives: 24.5 us -> 39.1 us  [the longest x1 24.5 us: body(): lax.all_to_all(jnp.broadcast_to(squares, (head_parts, parts, LANES)), 'he...]
    unnamed x18 -> x2, local copies, waits for them, and re-layouts: 6.8 us -> 0.01 us
    all_to_all x1, waiting for transfers between devices: 10.6 us -> 5.21 us  [body(): lax.all_to_all(local_state.reshape(seq_size, piece_rows, head_size), 'seq...]
    all_to_all x1 -> x0, starting transfers between devices: 3.66 us -> none  [body(): lax.all_to_all(prefixes, 'seq', 0, 0, tiled=True).reshape(state_type.shape)]
    all_to_all x1 -> x0, waiting for transfers between devices: 3.27 us -> none  [body(): lax.all_to_all(prefixes, 'seq', 0, 0, tiled=True).reshape(state_type.shape)]
    pallas_call x3, Pallas kernels: 10.5 us -> 9.17 us  [the longest x1 5.38 us: body(): pl.pallas_call(inner_kernel, in_specs=[hbm] * 4, out_specs=[vmem] * 3, ou...]
    pallas_call x1, Pallas kernels: 1.33 us -> 0.07 us  [body(): pl.pallas_call(functools.partial(scan_kernel, float(block_len)), in_specs...]
    pallas_call x1, Pallas kernels: 2.07 us -> 1.15 us  [body(): pl.pallas_call(functools.partial(norm_kernel, float(columns * head_parts)...]
  transfers between devices with their start and end apart: 2 -> 1, of which waited for: 2 -> 1; matrix products, arithmetic and copies ran while one was open for 0% -> 0% of each run, Pallas kernels for 7% -> 8%
where the time goes in v2:
time: 67.1 us; the launch traced here: 66.8 us
  blocking collectives  39.1 us (58%)
  starting transfers between devices  11.4 us (17%)
  Pallas kernels  10.4 us (15%)
  waiting for transfers between devices  5.21 us (8%)
  between operations  0.7 us (1%)
    all_to_all x1, blocking collectives, body(): lax.all_to_all(jnp.broadcast_to(squares, (head_parts, parts, LANES)), 'he...  24.5 us
    all_to_all x1, blocking collectives, body(): lax.all_to_all(prefixes, 'seq', 0, 0, tiled=True).reshape(state_type.shape)  14.6 us
    all_to_all x1, starting transfers between devices, body(): lax.all_to_all(local_state.reshape(seq_size, piece_rows, head_size), 'seq...  11.4 us
    pallas_call x1, Pallas kernels, body(): pl.pallas_call(inner_kernel, in_specs=[hbm] * 4, out_specs=[vmem] * 3, ou...  5.38 us
    all_to_all x1, waiting for transfers between devices, body(): lax.all_to_all(local_state.reshape(seq_size, piece_rows, head_size), 'seq...  5.21 us
    pallas_call x1, Pallas kernels, body(): pl.pallas_call(local_kernel, in_specs=[hbm] * 3, out_specs=vmem, out_shap...  2.99 us
  transfers between devices with their start and end apart: 1, of which 1 were waited for; matrix products, arithmetic and copies ran while one was open for 0% of the time, Pallas kernels for 8%

profile of v2, /device:TPU:1, one launch (start us, length us, event | category | flops | bytes accessed | tf_op | source)
XLA Modules:
  0.0 66.8 jit_solution(4315784838452392714)
XLA Ops:
  0.0 3.0 %local_state.1 = f32[4,128,128]{2,1,0:T(8,128)} custom-call(f32[4]{0:T(128)} %rate_hbm.3, bf16[1024,512]{1,0:T(8,128)(2,1)} %bitcast.9, bf16[1024,512]{1,0:T(8,128)(2,1)} %bitcast.11), custom_call_target="tpu_custom_call" | custom-call | flops 134217728 | bytes 2359296 | tf_op jit(solution)/shard_map/local_state/pallas_call | solution.py:192
  3.0 11.4 %all-to-all-start = ((f32[32,16,128]{2,1,0:T(8,128)}), f32[32,16,128]{2,1,0:T(8,128)S(1)}, u32[]{:S(2)}, u32[]{:S(2)}) async-start(f32[32,16,128]{2,1,0:T(8,128)} %bitcast.3), calls=%async_computation | async-start | bytes 524288 | tf_op jit(solution)/shard_map/all_to_all | solution.py:207
  15.0 5.4 %inner.1 = (f32[1024,512]{1,0:T(8,128)S(1)}, bf16[1024,512]{1,0:T(8,128)(2,1)S(1)}, f32[4,16,128]{2,1,0:T(8,128)S(1)}) custom-call(f32[4]{0:T(128)} %rate_hbm.3, bf16[1024,512]{1,0:T(8,128)(2,1)} %bitcast.13, bf16[1024,512]{1,0:T(8,128)(2,1)} %bitcast.10, bf16[1024,512]{1,0:T(8,128)(2,1)} %bitcast.12), custom_call_target="tpu_custom_call" | custom-call | flops 939524096 | bytes 8388608 | tf_op jit(solution)/shard_map/inner/pallas_call | solution.py:210
  20.4 5.2 %all-to-all-done.in_ref = f32[32,16,128]{2,1,0:T(8,128)S(1)} async-done(((f32[32,16,128]{2,1,0:T(8,128)}), f32[32,16,128]{2,1,0:T(8,128)S(1)}, u32[]{:S(2)}, u32[]{:S(2)}) %all-to-all-start) | async-done | bytes 262176 | tf_op jit(solution)/shard_map/all_to_all | solution.py:207
  25.6 0.1 scan.1
  25.7 0.0 copy-start
  25.7 14.6 %all_to_all.15 = f32[32,16,128]{2,1,0:T(8,128)S(1)} all-to-all(f32[32,16,128]{2,1,0:T(8,128)S(1)} %scan.1), channel_id=1, replica_groups=mesh['head'=16,'seq'=32] {'seq'}, dimensions={0} | all-to-all | bytes 524288 | tf_op jit(solution)/shard_map/all_to_all | solution.py:239
  40.4 0.8 %attend.1 = (f32[1024,512]{1,0:T(8,128)S(1)}, f32[8,128]{1,0:T(8,128)S(1)}) custom-call(bf16[1024,512]{1,0:T(8,128)(2,1)S(1)} %get-tuple-element.10.query_ref, f32[1024,512]{1,0:T(8,128)S(1)} %get-tuple-element.11.inner_ref, f32[4,16,128]{2,1,0:T(8,128)S(1)} %get-tuple-element.12.wide_ref, f32[4,128,128]{2,1,0:T(8,128)S(1)} %bitcast.7), custom_call_target="tpu_custom_call" | custom-call | tf_op jit(solution)/shard_map/attend/pallas_call | solution.py:241
  41.2 24.5 %all_to_all.16.squares_ref = f32[16,8,128]{2,1,0:T(8,128)S(1)} all-to-all(f32[16,8,128]{2,1,0:T(8,128)S(1)} %broadcast_in_dim.3), channel_id=1, replica_groups=mesh['head'=16,'seq'=32] {'head'}, dimensions={0} | all-to-all | bytes 131072 | tf_op jit(solution)/shard_map/all_to_all | solution.py:250
  65.7 0.0 copy-done
  65.7 1.1 %norm.1 = bf16[1024,512]{1,0:T(8,128)(2,1)} custom-call(f32[1024,512]{1,0:T(8,128)S(1)} %get-tuple-element.13.attended_ref, f32[16,8,128]{2,1,0:T(8,128)S(1)} %all_to_all.16.squares_ref, f32[1,512]{1,0:T(1,128)S(1)} %bitcast.8), custom_call_target="tpu_custom_call" | custom-call | tf_op jit(solution)/shard_map/norm/pallas_call | solution.py:253
  (1 shorter events, 0.0 us)
Async XLA Ops:
  3.0 22.6 %all-to-all-start = ((f32[32,16,128]{2,1,0:T(8,128)}), f32[32,16,128]{2,1,0:T(8,128)S(1)}, u32[]{:S(2)}, u32[]{:S(2)}) async-start(f32[32,16,128]{2,1,0:T(8,128)} %bitcast.3), calls=%async_computation | async-start | bytes 524288 | tf_op jit(solution)/shard_map/all_to_all | solution.py:207
  25.7 40.0 %copy-start = (f32[512]{0:T(512)S(1)}, f32[512]{0:T(512)}, u32[]{:S(2)}) copy-start(f32[512]{0:T(512)} %param.10) | copy-start | bytes 6148

commit v3 on v2

--- a/solution.py
+++ b/solution.py
@@ -10,6 +10,7 @@
 epsilon = 1e-05
 CHUNK = 256
 LANES = 128
+ROTATION = 10
 F32 = jnp.float32
 BF16 = jnp.bfloat16
 PARAMS = pltpu.CompilerParams(vmem_limit_bytes=16 * 2**20)
@@ -53,7 +54,9 @@
     return copies
 
 
-def local_kernel(rate_hbm, k_hbm, v_hbm, out_ref, rates, k_buf, v_buf, sems, rate_sem):
+def local_kernel(
+    rate_hbm, k_hbm, v_hbm, out_hbm, rates, k_buf, v_buf, out_buf, sems, rate_sem, out_sems
+):
     rate_copy = pltpu.make_async_copy(rate_hbm, rates, rate_sem)
     rate_copy.start()
     copies = head_copies((k_hbm, v_hbm), (k_buf, v_buf), sems)
@@ -61,6 +64,7 @@
     chunk = min(CHUNK, block_len)
     places = rows_of((chunk, head_size))
     rate_copy.wait()
+    out_copies = []
     for head in range(heads):
         rate = rates[head]
         scale = jnp.exp(-rate * (chunk - 1.0 - places))
@@ -72,7 +76,11 @@
             key = k_buf[head, start : start + chunk, :]
             pieces.append((key.astype(F32) * scale).astype(BF16))
             scale = scale * chunk_decay
-        out_ref[head] = dot(jnp.concatenate(pieces[::-1], axis=0), v_buf[head], 0, 0)
+        out_buf[head] = dot(jnp.concatenate(pieces[::-1], axis=0), v_buf[head], 0, 0)
+        out_copies.append(pltpu.make_async_copy(out_buf.at[head], out_hbm.at[head], out_sems.at[head]))
+        out_copies[-1].start()
+    for copy in out_copies:
+        copy.wait()
 
 
 def inner_kernel(
@@ -117,9 +125,10 @@
 def scan_kernel(block_len, wide_ref, offset_ref, in_ref, out_ref):
     count, rows, lanes = in_ref.shape
     heads = wide_ref.shape[0]
-    decay = jnp.exp(wide_ref[lax.axis_index("seq") * heads // count] * block_len)
+    mine = lax.rem(lax.axis_index("seq") + (count - ROTATION % count), count)
+    decay = jnp.exp(wide_ref[mine * heads // count] * block_len)
     state = jnp.zeros((rows, lanes), F32)
-    place = offset_ref[0]
+    place = lax.rem(offset_ref[0] + (count - ROTATION % count), count)
     for _ in range(count):
         out_ref[place] = state
         state = decay * state + in_ref[place]
@@ -189,12 +198,16 @@
     buffer = pltpu.VMEM((heads, block_len, head_size), BF16)
     rates = pltpu.SMEM((heads,), F32)
 
+    dma = pltpu.SemaphoreType.DMA
     local_state = pl.pallas_call(
         local_kernel,
         in_specs=[hbm] * 3,
-        out_specs=vmem,
+        out_specs=hbm,
         out_shape=state_type,
-        scratch_shapes=[rates, buffer, buffer, pltpu.SemaphoreType.DMA((2, heads)), pltpu.SemaphoreType.DMA],
+        scratch_shapes=[
+            rates, buffer, buffer, pltpu.VMEM(state_type.shape, F32),
+            dma((2, heads)), dma, dma((heads,)),
+        ],
         name="local_state",
         compiler_params=PARAMS,
         cost_estimate=pl.CostEstimate(
@@ -204,9 +217,13 @@
         ),
     )(decay_rate, keys, values)
 
-    pieces = lax.all_to_all(
-        local_state.reshape(seq_size, piece_rows, head_size), "seq", 0, 0, tiled=True
-    )
+    seq_order = [(i + ROTATION) % seq_size for i in range(seq_size)]
+    head_order = [*range(0, head_parts, 2), *range(1, head_parts, 2)]
+
+    def exchange(array):
+        return lax.all_to_all(array, "seq", 0, 0, tiled=True, axis_index_groups=[seq_order])
+
+    pieces = exchange(local_state.reshape(seq_size, piece_rows, head_size))
     inner, query_copy, wide_rates = pl.pallas_call(
         inner_kernel,
         in_specs=[hbm] * 4,
@@ -216,9 +233,7 @@
             jax.ShapeDtypeStruct((block_len, columns), BF16),
             jax.ShapeDtypeStruct((heads, piece_rows, head_size), F32),
         ],
-        scratch_shapes=[
-            rates, buffer, buffer, buffer, pltpu.SemaphoreType.DMA((3, heads)), pltpu.SemaphoreType.DMA,
-        ],
+        scratch_shapes=[rates, buffer, buffer, buffer, dma((3, heads)), dma],
         name="inner",
         compiler_params=PARAMS,
         cost_estimate=pl.CostEstimate(
@@ -236,7 +251,7 @@
         name="scan",
         compiler_params=PARAMS,
     )(wide_rates, offsets, pieces)
-    incoming = lax.all_to_all(prefixes, "seq", 0, 0, tiled=True).reshape(state_type.shape)
+    incoming = exchange(prefixes).reshape(state_type.shape)
 
     attended, squares = pl.pallas_call(
         attend_kernel,
@@ -248,7 +263,12 @@
     )(query_copy, inner, wide_rates, incoming)
 
     gathered = lax.all_to_all(
-        jnp.broadcast_to(squares, (head_parts, parts, LANES)), "head", 0, 0, tiled=True
+        jnp.broadcast_to(squares, (head_parts, parts, LANES)),
+        "head",
+        0,
+        0,
+        tiled=True,
+        axis_index_groups=[head_order],
     )
     normed = pl.pallas_call(
         functools.partial(norm_kernel, float(columns * head_parts)),

time: 67.1 us -> 63.9 us (0.952)
  blocking collectives: 39.1 us -> 37.3 us
  waiting for transfers between devices: 5.21 us -> 3.62 us
    all_to_all x1, waiting for transfers between devices: 5.21 us -> 3.62 us  [exchange(): lax.all_to_all(array, 'seq', 0, 0, tiled=True, axis_index_groups=[seq_ord...]
    all_to_all x1, blocking collectives: 14.6 us -> 13.6 us  [exchange(): lax.all_to_all(array, 'seq', 0, 0, tiled=True, axis_index_groups=[seq_ord...]
    all_to_all x1, blocking collectives: 24.5 us -> 23.8 us  [body(): lax.all_to_all(jnp.broadcast_to(squares, (head_parts, parts, LANES)), 'he...]
where the time goes in v3:
time: 63.9 us; the launch traced here: 63.6 us
  blocking collectives  37.3 us (58%)
  starting transfers between devices  11.6 us (18%)
  Pallas kernels  10.4 us (16%)
  waiting for transfers between devices  3.62 us (6%)
  between operations  0.7 us (1%)
    all_to_all x1, blocking collectives, body(): lax.all_to_all(jnp.broadcast_to(squares, (head_parts, parts, LANES)), 'he...  23.8 us
    all_to_all x1, blocking collectives, exchange(): lax.all_to_all(array, 'seq', 0, 0, tiled=True, axis_index_groups=[seq_ord...  13.6 us
    all_to_all x1, starting transfers between devices, exchange(): lax.all_to_all(array, 'seq', 0, 0, tiled=True, axis_index_groups=[seq_ord...  11.6 us
    pallas_call x1, Pallas kernels, body(): pl.pallas_call(inner_kernel, in_specs=[hbm] * 4, out_specs=[vmem] * 3, ou...  5.39 us
    all_to_all x1, waiting for transfers between devices, exchange(): lax.all_to_all(array, 'seq', 0, 0, tiled=True, axis_index_groups=[seq_ord...  3.62 us
    pallas_call x1, Pallas kernels, body(): pl.pallas_call(local_kernel, in_specs=[hbm] * 3, out_specs=hbm, out_shape...  2.95 us
  transfers between devices with their start and end apart: 1, of which 1 were waited for; matrix products, arithmetic and copies ran while one was open for 0% of the time, Pallas kernels for 8%

profile of v3, /device:TPU:1, one launch (start us, length us, event | category | flops | bytes accessed | tf_op | source)
XLA Modules:
  0.0 63.6 jit_solution(3937978430730703855)
XLA Ops:
  0.0 3.0 %local_state.1 = f32[4,128,128]{2,1,0:T(8,128)} custom-call(f32[4]{0:T(128)} %rate_hbm.3, bf16[1024,512]{1,0:T(8,128)(2,1)} %bitcast.9, bf16[1024,512]{1,0:T(8,128)(2,1)} %bitcast.11), custom_call_target="tpu_custom_call" | custom-call | flops 134217728 | bytes 2359296 | tf_op jit(solution)/shard_map/local_state/pallas_call | solution.py:202
  3.0 11.6 %all-to-all-start = ((f32[32,16,128]{2,1,0:T(8,128)}), f32[32,16,128]{2,1,0:T(8,128)S(1)}, u32[]{:S(2)}, u32[]{:S(2)}) async-start(f32[32,16,128]{2,1,0:T(8,128)} %bitcast.3), calls=%async_computation | async-start | bytes 524288 | tf_op jit(solution)/shard_map/all_to_all | solution.py:224
  15.2 5.4 %inner.1 = (f32[1024,512]{1,0:T(8,128)S(1)}, bf16[1024,512]{1,0:T(8,128)(2,1)S(1)}, f32[4,16,128]{2,1,0:T(8,128)S(1)}) custom-call(f32[4]{0:T(128)} %rate_hbm.3, bf16[1024,512]{1,0:T(8,128)(2,1)} %bitcast.13, bf16[1024,512]{1,0:T(8,128)(2,1)} %bitcast.10, bf16[1024,512]{1,0:T(8,128)(2,1)} %bitcast.12), custom_call_target="tpu_custom_call" | custom-call | flops 939524096 | bytes 8388608 | tf_op jit(solution)/shard_map/inner/pallas_call | solution.py:227
  20.6 3.6 %all-to-all-done.in_ref = f32[32,16,128]{2,1,0:T(8,128)S(1)} async-done(((f32[32,16,128]{2,1,0:T(8,128)}), f32[32,16,128]{2,1,0:T(8,128)S(1)}, u32[]{:S(2)}, u32[]{:S(2)}) %all-to-all-start) | async-done | bytes 262176 | tf_op jit(solution)/shard_map/all_to_all | solution.py:224
  24.2 0.1 scan.1
  24.3 0.0 copy-start
  24.3 13.6 %all_to_all.15 = f32[32,16,128]{2,1,0:T(8,128)S(1)} all-to-all(f32[32,16,128]{2,1,0:T(8,128)S(1)} %scan.1), channel_id=1, replica_groups={{10,11,12,13,14,15,16,17,18,19,20,21,22,23,24,25,26,27,28,29,30,31,0,1,..., dimensions={0} | all-to-all | bytes 524288 | tf_op jit(solution)/shard_map/all_to_all | solution.py:224
  37.9 0.8 %attend.1 = (f32[1024,512]{1,0:T(8,128)S(1)}, f32[8,128]{1,0:T(8,128)S(1)}) custom-call(bf16[1024,512]{1,0:T(8,128)(2,1)S(1)} %get-tuple-element.10.query_ref, f32[1024,512]{1,0:T(8,128)S(1)} %get-tuple-element.11.inner_ref, f32[4,16,128]{2,1,0:T(8,128)S(1)} %get-tuple-element.12.wide_ref, f32[4,128,128]{2,1,0:T(8,128)S(1)} %bitcast.7), custom_call_target="tpu_custom_call" | custom-call | tf_op jit(solution)/shard_map/attend/pallas_call | solution.py:256
  38.7 23.8 %all_to_all.16.squares_ref = f32[16,8,128]{2,1,0:T(8,128)S(1)} all-to-all(f32[16,8,128]{2,1,0:T(8,128)S(1)} %broadcast_in_dim.3), channel_id=1, replica_groups={{0,64,128,192,256,320,384,448,32,96,160,224,288,352,416,480},{1,65,129,..., dimensions={0} | all-to-all | bytes 131072 | tf_op jit(solution)/shard_map/all_to_all | solution.py:265
  62.5 0.0 copy-done
  62.5 1.1 %norm.1 = bf16[1024,512]{1,0:T(8,128)(2,1)} custom-call(f32[1024,512]{1,0:T(8,128)S(1)} %get-tuple-element.13.attended_ref, f32[16,8,128]{2,1,0:T(8,128)S(1)} %all_to_all.16.squares_ref, f32[1,512]{1,0:T(1,128)S(1)} %bitcast.8), custom_call_target="tpu_custom_call" | custom-call | tf_op jit(solution)/shard_map/norm/pallas_call | solution.py:273
  (1 shorter events, 0.0 us)
Async XLA Ops:
  3.0 21.3 %all-to-all-start = ((f32[32,16,128]{2,1,0:T(8,128)}), f32[32,16,128]{2,1,0:T(8,128)S(1)}, u32[]{:S(2)}, u32[]{:S(2)}) async-start(f32[32,16,128]{2,1,0:T(8,128)} %bitcast.3), calls=%async_computation | async-start | bytes 524288 | tf_op jit(solution)/shard_map/all_to_all | solution.py:224
  24.3 38.2 %copy-start = (f32[512]{0:T(512)S(1)}, f32[512]{0:T(512)}, u32[]{:S(2)}) copy-start(f32[512]{0:T(512)} %param.10) | copy-start | bytes 6148

commit v4 on v3

--- a/solution.py
+++ b/solution.py
@@ -10,7 +10,8 @@
 epsilon = 1e-05
 CHUNK = 256
 LANES = 128
-ROTATION = 10
+ROTATION = 21
+HEAD_START = 10
 F32 = jnp.float32
 BF16 = jnp.bfloat16
 PARAMS = pltpu.CompilerParams(vmem_limit_bytes=16 * 2**20)
@@ -218,7 +219,10 @@
     )(decay_rate, keys, values)
 
     seq_order = [(i + ROTATION) % seq_size for i in range(seq_size)]
-    head_order = [*range(0, head_parts, 2), *range(1, head_parts, 2)]
+    half = head_parts // 2
+    head_order = [
+        (HEAD_START + 2 * k) % head_parts + part for part in (1, 0) for k in range(half)
+    ]
 
     def exchange(array):
         return lax.all_to_all(array, "seq", 0, 0, tiled=True, axis_index_groups=[seq_order])

time: 63.9 us -> 53.9 us (0.84)
  blocking collectives: 37.3 us -> 28.8 us
  waiting for transfers between devices: 3.62 us -> 0.72 us
  starting transfers between devices: 11.6 us -> 12.9 us
    all_to_all x1, blocking collectives: 23.8 us -> 15.3 us  [body(): lax.all_to_all(jnp.broadcast_to(squares, (head_parts, parts, LANES)), 'he...]
    all_to_all x1, waiting for transfers between devices: 3.62 us -> 0.72 us  [exchange(): lax.all_to_all(array, 'seq', 0, 0, tiled=True, axis_index_groups=[seq_ord...]
    all_to_all x1, starting transfers between devices: 11.6 us -> 12.9 us  [exchange(): lax.all_to_all(array, 'seq', 0, 0, tiled=True, axis_index_groups=[seq_ord...]
  transfers between devices with their start and end apart: 1 -> 1, of which waited for: 1 -> 1; matrix products, arithmetic and copies ran while one was open for 0% -> 0% of each run, Pallas kernels for 8% -> 10%
where the time goes in v4:
time: 53.9 us; the launch traced here: 53.6 us
  blocking collectives  28.8 us (53%)
  starting transfers between devices  12.9 us (24%)
  Pallas kernels  10.4 us (19%)
  waiting for transfers between devices  0.72 us (1%)
  between operations  0.7 us (1%)
    all_to_all x1, blocking collectives, body(): lax.all_to_all(jnp.broadcast_to(squares, (head_parts, parts, LANES)), 'he...  15.3 us
    all_to_all x1, blocking collectives, exchange(): lax.all_to_all(array, 'seq', 0, 0, tiled=True, axis_index_groups=[seq_ord...  13.6 us
    all_to_all x1, starting transfers between devices, exchange(): lax.all_to_all(array, 'seq', 0, 0, tiled=True, axis_index_groups=[seq_ord...  12.9 us
    pallas_call x1, Pallas kernels, body(): pl.pallas_call(inner_kernel, in_specs=[hbm] * 4, out_specs=[vmem] * 3, ou...  5.39 us
    pallas_call x1, Pallas kernels, body(): pl.pallas_call(local_kernel, in_specs=[hbm] * 3, out_specs=hbm, out_shape...  2.95 us
    pallas_call x1, Pallas kernels, body(): pl.pallas_call(functools.partial(norm_kernel, float(columns * head_parts)...  1.15 us
  transfers between devices with their start and end apart: 1, of which 1 were waited for; matrix products, arithmetic and copies ran while one was open for 0% of the time, Pallas kernels for 10%

profile of v4, /device:TPU:1, one launch (start us, length us, event | category | flops | bytes accessed | tf_op | source)
XLA Modules:
  0.0 53.6 jit_solution(8897571614958960318)
XLA Ops:
  0.0 3.0 %local_state.1 = f32[4,128,128]{2,1,0:T(8,128)} custom-call(f32[4]{0:T(128)} %rate_hbm.3, bf16[1024,512]{1,0:T(8,128)(2,1)} %bitcast.9, bf16[1024,512]{1,0:T(8,128)(2,1)} %bitcast.11), custom_call_target="tpu_custom_call" | custom-call | flops 134217728 | bytes 2359296 | tf_op jit(solution)/shard_map/local_state/pallas_call | solution.py:203
  3.0 12.9 %all-to-all-start = ((f32[32,16,128]{2,1,0:T(8,128)}), f32[32,16,128]{2,1,0:T(8,128)S(1)}, u32[]{:S(2)}, u32[]{:S(2)}) async-start(f32[32,16,128]{2,1,0:T(8,128)} %bitcast.3), calls=%async_computation | async-start | bytes 524288 | tf_op jit(solution)/shard_map/all_to_all | solution.py:228
  16.6 5.4 %inner.1 = (f32[1024,512]{1,0:T(8,128)S(1)}, bf16[1024,512]{1,0:T(8,128)(2,1)S(1)}, f32[4,16,128]{2,1,0:T(8,128)S(1)}) custom-call(f32[4]{0:T(128)} %rate_hbm.3, bf16[1024,512]{1,0:T(8,128)(2,1)} %bitcast.13, bf16[1024,512]{1,0:T(8,128)(2,1)} %bitcast.10, bf16[1024,512]{1,0:T(8,128)(2,1)} %bitcast.12), custom_call_target="tpu_custom_call" | custom-call | flops 939524096 | bytes 8388608 | tf_op jit(solution)/shard_map/inner/pallas_call | solution.py:231
  22.0 0.7 %all-to-all-done.in_ref = f32[32,16,128]{2,1,0:T(8,128)S(1)} async-done(((f32[32,16,128]{2,1,0:T(8,128)}), f32[32,16,128]{2,1,0:T(8,128)S(1)}, u32[]{:S(2)}, u32[]{:S(2)}) %all-to-all-start) | async-done | bytes 262176 | tf_op jit(solution)/shard_map/all_to_all | solution.py:228
  22.7 0.1 scan.1
  22.8 0.0 copy-start
  22.8 13.6 %all_to_all.15 = f32[32,16,128]{2,1,0:T(8,128)S(1)} all-to-all(f32[32,16,128]{2,1,0:T(8,128)S(1)} %scan.1), channel_id=1, replica_groups={{21,22,23,24,25,26,27,28,29,30,31,0,1,2,3,4,5,6,7,8,9,10,11,12,13,14,15..., dimensions={0} | all-to-all | bytes 524288 | tf_op jit(solution)/shard_map/all_to_all | solution.py:228
  36.3 0.8 %attend.1 = (f32[1024,512]{1,0:T(8,128)S(1)}, f32[8,128]{1,0:T(8,128)S(1)}) custom-call(bf16[1024,512]{1,0:T(8,128)(2,1)S(1)} %get-tuple-element.10.query_ref, f32[1024,512]{1,0:T(8,128)S(1)} %get-tuple-element.11.inner_ref, f32[4,16,128]{2,1,0:T(8,128)S(1)} %get-tuple-element.12.wide_ref, f32[4,128,128]{2,1,0:T(8,128)S(1)} %bitcast.7), custom_call_target="tpu_custom_call" | custom-call | tf_op jit(solution)/shard_map/attend/pallas_call | solution.py:260
  37.1 15.3 %all_to_all.16.squares_ref = f32[16,8,128]{2,1,0:T(8,128)S(1)} all-to-all(f32[16,8,128]{2,1,0:T(8,128)S(1)} %broadcast_in_dim.3), channel_id=1, replica_groups={{352,416,480,32,96,160,224,288,320,384,448,0,64,128,192,256},{353,417,4..., dimensions={0} | all-to-all | bytes 131072 | tf_op jit(solution)/shard_map/all_to_all | solution.py:269
  52.4 0.0 copy-done
  52.4 1.1 %norm.1 = bf16[1024,512]{1,0:T(8,128)(2,1)} custom-call(f32[1024,512]{1,0:T(8,128)S(1)} %get-tuple-element.13.attended_ref, f32[16,8,128]{2,1,0:T(8,128)S(1)} %all_to_all.16.squares_ref, f32[1,512]{1,0:T(1,128)S(1)} %bitcast.8), custom_call_target="tpu_custom_call" | custom-call | tf_op jit(solution)/shard_map/norm/pallas_call | solution.py:277
  (1 shorter events, 0.0 us)
Async XLA Ops:
  3.0 19.7 %all-to-all-start = ((f32[32,16,128]{2,1,0:T(8,128)}), f32[32,16,128]{2,1,0:T(8,128)S(1)}, u32[]{:S(2)}, u32[]{:S(2)}) async-start(f32[32,16,128]{2,1,0:T(8,128)} %bitcast.3), calls=%async_computation | async-start | bytes 524288 | tf_op jit(solution)/shard_map/all_to_all | solution.py:228
  22.8 29.7 %copy-start = (f32[512]{0:T(512)S(1)}, f32[512]{0:T(512)}, u32[]{:S(2)}) copy-start(f32[512]{0:T(512)} %param.10) | copy-start | bytes 6148

commit v5 on v4

--- a/solution.py
+++ b/solution.py
@@ -56,7 +56,7 @@
 
 
 def local_kernel(
-    rate_hbm, k_hbm, v_hbm, out_hbm, rates, k_buf, v_buf, out_buf, sems, rate_sem, out_sems
+    rate_hbm, k_hbm, v_hbm, out_ref, wide_ref, rates, k_buf, v_buf, sems, rate_sem
 ):
     rate_copy = pltpu.make_async_copy(rate_hbm, rates, rate_sem)
     rate_copy.start()
@@ -65,9 +65,9 @@
     chunk = min(CHUNK, block_len)
     places = rows_of((chunk, head_size))
     rate_copy.wait()
-    out_copies = []
     for head in range(heads):
         rate = rates[head]
+        wide_ref[head] = jnp.full(wide_ref.shape[1:], -rate, F32)
         scale = jnp.exp(-rate * (chunk - 1.0 - places))
         chunk_decay = jnp.exp(jnp.full((chunk, head_size), -rate * chunk, F32))
         for copy in copies[head]:
@@ -77,15 +77,11 @@
             key = k_buf[head, start : start + chunk, :]
             pieces.append((key.astype(F32) * scale).astype(BF16))
             scale = scale * chunk_decay
-        out_buf[head] = dot(jnp.concatenate(pieces[::-1], axis=0), v_buf[head], 0, 0)
-        out_copies.append(pltpu.make_async_copy(out_buf.at[head], out_hbm.at[head], out_sems.at[head]))
-        out_copies[-1].start()
-    for copy in out_copies:
-        copy.wait()
+        out_ref[head] = dot(jnp.concatenate(pieces[::-1], axis=0), v_buf[head], 0, 0)
 
 
 def inner_kernel(
-    rate_hbm, q_hbm, k_hbm, v_hbm, out_ref, query_ref, wide_ref,
+    rate_hbm, q_hbm, k_hbm, v_hbm, after, out_ref, query_ref,
     rates, q_buf, k_buf, v_buf, sems, rate_sem,
 ):
     rate_copy = pltpu.make_async_copy(rate_hbm, rates, rate_sem)
@@ -104,7 +100,6 @@
         key_scale = jnp.exp(-rate * (chunk - 1.0 - places))
         query_scale = jnp.exp(-rate * (places + 1.0))
         chunk_decay = jnp.exp(jnp.full((head_size, head_size), -rate * chunk, F32))
-        wide_ref[head] = jnp.full(wide_ref.shape[1:], -rate, F32)
         for copy in copies[head]:
             copy.wait()
         state = None
@@ -200,15 +195,13 @@
     rates = pltpu.SMEM((heads,), F32)
 
     dma = pltpu.SemaphoreType.DMA
-    local_state = pl.pallas_call(
+    wide_type_rates = jax.ShapeDtypeStruct((heads, piece_rows, head_size), F32)
+    local_state, wide_rates = pl.pallas_call(
         local_kernel,
         in_specs=[hbm] * 3,
-        out_specs=hbm,
-        out_shape=state_type,
-        scratch_shapes=[
-            rates, buffer, buffer, pltpu.VMEM(state_type.shape, F32),
-            dma((2, heads)), dma, dma((heads,)),
-        ],
+        out_specs=[vmem, vmem],
+        out_shape=[state_type, wide_type_rates],
+        scratch_shapes=[rates, buffer, buffer, dma((2, heads)), dma],
         name="local_state",
         compiler_params=PARAMS,
         cost_estimate=pl.CostEstimate(
@@ -228,25 +221,6 @@
         return lax.all_to_all(array, "seq", 0, 0, tiled=True, axis_index_groups=[seq_order])
 
     pieces = exchange(local_state.reshape(seq_size, piece_rows, head_size))
-    inner, query_copy, wide_rates = pl.pallas_call(
-        inner_kernel,
-        in_specs=[hbm] * 4,
-        out_specs=[vmem] * 3,
-        out_shape=[
-            wide_type,
-            jax.ShapeDtypeStruct((block_len, columns), BF16),
-            jax.ShapeDtypeStruct((heads, piece_rows, head_size), F32),
-        ],
-        scratch_shapes=[rates, buffer, buffer, buffer, dma((3, heads)), dma],
-        name="inner",
-        compiler_params=PARAMS,
-        cost_estimate=pl.CostEstimate(
-            flops=2 * block_len * columns * (2 * CHUNK + 3 * head_size),
-            bytes_accessed=16 * block_len * columns,
-            transcendentals=CHUNK * CHUNK * heads,
-        ),
-    )(decay_rate, queries, keys, values)
-
     prefixes = pl.pallas_call(
         functools.partial(scan_kernel, float(block_len)),
         in_specs=[vmem, smem, vmem],
@@ -255,6 +229,24 @@
         name="scan",
         compiler_params=PARAMS,
     )(wide_rates, offsets, pieces)
+    inner, query_copy = pl.pallas_call(
+        inner_kernel,
+        in_specs=[hbm] * 4 + [pl.BlockSpec(memory_space=pl.ANY)],
+        out_specs=[vmem] * 2,
+        out_shape=[
+            wide_type,
+            jax.ShapeDtypeStruct((block_len, columns), BF16),
+        ],
+        scratch_shapes=[rates, buffer, buffer, buffer, dma((3, heads)), dma],
+        name="inner",
+        compiler_params=PARAMS,
+        cost_estimate=pl.CostEstimate(
+            flops=2 * block_len * columns * (2 * CHUNK + 3 * head_size),
+            bytes_accessed=16 * block_len * columns,
+            transcendentals=CHUNK * CHUNK * heads,
+        ),
+    )(decay_rate, queries, keys, values, prefixes)
+
     incoming = exchange(prefixes).reshape(state_type.shape)
 
     attended, squares = pl.pallas_call(

time: 53.9 us -> 54.8 us (1.017)
  blocking collectives: 28.8 us -> 15.3 us
  starting transfers between devices: 12.9 us -> 19.9 us
  waiting for transfers between devices: 0.72 us -> 7.46 us
  Pallas kernels: 10.4 us -> 11.1 us
    all_to_all x1 -> x0, blocking collectives: 13.6 us -> none  [exchange(): lax.all_to_all(array, 'seq', 0, 0, tiled=True, axis_index_groups=[seq_ord...]
    all_to_all x1 -> x2, starting transfers between devices: 12.9 us -> 19.9 us  [exchange(): lax.all_to_all(array, 'seq', 0, 0, tiled=True, axis_index_groups=[seq_ord...]
    all_to_all x1 -> x2, waiting for transfers between devices: 0.72 us -> 7.46 us  [exchange(): lax.all_to_all(array, 'seq', 0, 0, tiled=True, axis_index_groups=[seq_ord...]
    pallas_call x1, Pallas kernels: 0.07 us -> 0.78 us  [body(): pl.pallas_call(functools.partial(scan_kernel, float(block_len)), in_specs...]
  transfers between devices with their start and end apart: 1 -> 2, of which waited for: 1 -> 2; matrix products, arithmetic and copies ran while one was open for 0% -> 0% of each run, Pallas kernels for 10% -> 10%
where the time goes in v5:
time: 54.8 us; the launch traced here: 54.5 us
  starting transfers between devices  19.9 us (36%)
  blocking collectives  15.3 us (28%)
  Pallas kernels  11.1 us (20%)
  waiting for transfers between devices  7.46 us (14%)
  between operations  0.7 us (1%)
    all_to_all x2, starting transfers between devices, exchange(): lax.all_to_all(array, 'seq', 0, 0, tiled=True, axis_index_groups=[seq_ord...  19.9 us
    all_to_all x1, blocking collectives, body(): lax.all_to_all(jnp.broadcast_to(squares, (head_parts, parts, LANES)), 'he...  15.3 us
    all_to_all x2, waiting for transfers between devices, exchange(): lax.all_to_all(array, 'seq', 0, 0, tiled=True, axis_index_groups=[seq_ord...  7.46 us
    pallas_call x1, Pallas kernels, body(): pl.pallas_call(inner_kernel, in_specs=[hbm] * 4 + [pl.BlockSpec(memory_sp...  5.4 us
    pallas_call x1, Pallas kernels, body(): pl.pallas_call(local_kernel, in_specs=[hbm] * 3, out_specs=[vmem, vmem],...  3 us
    pallas_call x1, Pallas kernels, body(): pl.pallas_call(functools.partial(norm_kernel, float(columns * head_parts)...  1.15 us
  transfers between devices with their start and end apart: 2, of which 2 were waited for; matrix products, arithmetic and copies ran while one was open for 0% of the time, Pallas kernels for 10%

profile of v5, /device:TPU:1, one launch (start us, length us, event | category | flops | bytes accessed | tf_op | source)
XLA Modules:
  0.0 54.5 jit_solution(13323144250776539231)
XLA Ops:
  0.0 3.0 %local_state.1 = (f32[4,128,128]{2,1,0:T(8,128)}, f32[4,16,128]{2,1,0:T(8,128)S(1)}) custom-call(f32[4]{0:T(128)} %rate_hbm.3, bf16[1024,512]{1,0:T(8,128)(2,1)} %bitcast.9, bf16[1024,512]{1,0:T(8,128)(2,1)} %bitcast.11), custom_call_target="tpu_custom_call" | custom-call | flops 134217728 | bytes 2359296 | tf_op jit(solution)/shard_map/local_state/pallas_call | solution.py:199
  3.0 12.9 %all-to-all-start = ((f32[32,16,128]{2,1,0:T(8,128)}), f32[32,16,128]{2,1,0:T(8,128)S(1)}, u32[]{:S(2)}, u32[]{:S(2)}) async-start(f32[32,16,128]{2,1,0:T(8,128)} %bitcast.3), calls=%async_computation | async-start | bytes 524288 | tf_op jit(solution)/shard_map/all_to_all | solution.py:221
  16.6 6.1 %all-to-all-done.in_ref = f32[32,16,128]{2,1,0:T(8,128)S(1)} async-done(((f32[32,16,128]{2,1,0:T(8,128)}), f32[32,16,128]{2,1,0:T(8,128)S(1)}, u32[]{:S(2)}, u32[]{:S(2)}) %all-to-all-start) | async-done | bytes 262176 | tf_op jit(solution)/shard_map/all_to_all | solution.py:221
  22.7 0.8 %scan.1.after = f32[32,16,128]{2,1,0:T(8,128)} custom-call(f32[4,16,128]{2,1,0:T(8,128)S(1)} %get-tuple-element.11.wide_ref, s32[1]{0:T(128)S(6)} %copy.7.offset_ref, f32[32,16,128]{2,1,0:T(8,128)S(1)} %all-to-all-done.in_ref), custom_call_target="tpu_custom_call" | custom-call | tf_op jit(solution)/shard_map/scan/pallas_call | solution.py:224
  23.5 7.0 %all-to-all-start.1 = ((f32[32,16,128]{2,1,0:T(8,128)}), f32[32,16,128]{2,1,0:T(8,128)S(1)}, u32[]{:S(2)}, u32[]{:S(2)}) async-start(f32[32,16,128]{2,1,0:T(8,128)} %scan.1.after), calls=%async_computation.1 | async-start | bytes 524288 | tf_op jit(solution)/shard_map/all_to_all | solution.py:221
  30.5 5.4 %inner.1 = (f32[1024,512]{1,0:T(8,128)S(1)}, bf16[1024,512]{1,0:T(8,128)(2,1)S(1)}) custom-call(f32[4]{0:T(128)} %rate_hbm.3, bf16[1024,512]{1,0:T(8,128)(2,1)} %bitcast.13, bf16[1024,512]{1,0:T(8,128)(2,1)} %bitcast.10, bf16[1024,512]{1,0:T(8,128)(2,1)} %bitcast.12, f32[32,16,128]{2,1,0:T(8,128)} %scan.1.after), custom_call_target="tpu_custom_call" | custom-call | flops 939524096 | bytes 8388608 | tf_op jit(solution)/shard_map/inner/pallas_call | solution.py:232
  35.9 0.0 copy-start
  35.9 1.3 %all-to-all-done.1 = f32[32,16,128]{2,1,0:T(8,128)S(1)} async-done(((f32[32,16,128]{2,1,0:T(8,128)}), f32[32,16,128]{2,1,0:T(8,128)S(1)}, u32[]{:S(2)}, u32[]{:S(2)}) %all-to-all-start.1) | async-done | bytes 262176 | tf_op jit(solution)/shard_map/all_to_all | solution.py:221
  37.3 0.8 %attend.1 = (f32[1024,512]{1,0:T(8,128)S(1)}, f32[8,128]{1,0:T(8,128)S(1)}) custom-call(bf16[1024,512]{1,0:T(8,128)(2,1)S(1)} %get-tuple-element.13.query_ref, f32[1024,512]{1,0:T(8,128)S(1)} %get-tuple-element.14.inner_ref, f32[4,16,128]{2,1,0:T(8,128)S(1)} %get-tuple-element.11.wide_ref, f32[4,128,128]{2,1,0:T(8,128)S(1)} %bitcast.7), custom_call_target="tpu_custom_call" | custom-call | tf_op jit(solution)/shard_map/attend/pallas_call | solution.py:252
  38.1 15.3 %all_to_all.15.squares_ref = f32[16,8,128]{2,1,0:T(8,128)S(1)} all-to-all(f32[16,8,128]{2,1,0:T(8,128)S(1)} %broadcast_in_dim.3), channel_id=1, replica_groups={{352,416,480,32,96,160,224,288,320,384,448,0,64,128,192,256},{353,417,4..., dimensions={0} | all-to-all | bytes 131072 | tf_op jit(solution)/shard_map/all_to_all | solution.py:261
  53.3 0.0 copy-done
  53.4 1.1 %norm.1 = bf16[1024,512]{1,0:T(8,128)(2,1)} custom-call(f32[1024,512]{1,0:T(8,128)S(1)} %get-tuple-element.15.attended_ref, f32[16,8,128]{2,1,0:T(8,128)S(1)} %all_to_all.15.squares_ref, f32[1,512]{1,0:T(1,128)S(1)} %bitcast.8), custom_call_target="tpu_custom_call" | custom-call | tf_op jit(solution)/shard_map/norm/pallas_call | solution.py:269
  (1 shorter events, 0.0 us)
Async XLA Ops:
  3.0 19.7 %all-to-all-start = ((f32[32,16,128]{2,1,0:T(8,128)}), f32[32,16,128]{2,1,0:T(8,128)S(1)}, u32[]{:S(2)}, u32[]{:S(2)}) async-start(f32[32,16,128]{2,1,0:T(8,128)} %bitcast.3), calls=%async_computation | async-start | bytes 524288 | tf_op jit(solution)/shard_map/all_to_all | solution.py:221
  23.5 13.8 %all-to-all-start.1 = ((f32[32,16,128]{2,1,0:T(8,128)}), f32[32,16,128]{2,1,0:T(8,128)S(1)}, u32[]{:S(2)}, u32[]{:S(2)}) async-start(f32[32,16,128]{2,1,0:T(8,128)} %scan.1.after), calls=%async_computation.1 | async-start | bytes 524288 | tf_op jit(solution)/shard_map/all_to_all | solution.py:221
  35.9 17.5 %copy-start = (f32[512]{0:T(512)S(1)}, f32[512]{0:T(512)}, u32[]{:S(2)}) copy-start(f32[512]{0:T(512)} %param.10) | copy-start | bytes 6148
